TPU v7x, 256 devices: a whole 4x4x8 slice. The times are simulated.
256 devices in a mesh: src: 32 (over x, z_lo, y), hid: 8 (over z_hi, core).
Axes of the slice: x: 4, y: 4, z: 8 (z_hi: 4, z_lo: 2; z = z_hi * 2 + z_lo), core: 2. Of those that a mesh axis runs over, the one named last changes fastest.
Arguments:
- source_field: float32 [256, 2, 98, 128], P('src'), may hold values from -36 to 36
- hidden_gain: float32 [98], replicated, may hold values from 0.1 to 1.9
- enc_tiles: float32 [8192, 128, 128], P(('src', 'hid')), may hold values from -0.25 to 0.25
- enc_src_block: int32 [8192], P(('src', 'hid')), may hold values from 0 to 255, as said below
- enc_hid_block: int32 [8192], P(('src', 'hid')), may hold values from 0 to 255, as said below
- enc_count: int32 [256], P(('src', 'hid')), may hold values from 1 to 32, as said below
- dec_tiles: float32 [8192, 128, 128], P(('src', 'hid')), may hold values from -0.15625 to 0.15625
- dec_src_block: int32 [8192], P(('src', 'hid')), may hold values from 0 to 255, as said below
- dec_hid_block: int32 [8192], P(('src', 'hid')), may hold values from 0 to 255, as said below
- dec_count: int32 [256], P(('src', 'hid')), may hold values from 1 to 32, as said below
Outputs:
- returned: float32 [256, 2, 98, 128], P('src')
- channel_rms: float32 [98], replicated
Inputs may be any that keep to these rules, and one draw needn't show every extreme that they name: `enc_src_block`: the 32 entries starting at (s * 8 + h) * 32 lie in s * 8 to (s + 1) * 8 - 1. `enc_hid_block`: the 32 entries starting at (s * 8 + h) * 32 lie in h * 32 to (h + 1) * 32 - 1; within these entries no pair (enc_src_block, enc_hid_block) repeats. `enc_count`: entry s * 8 + h counts the live slots of that group; it equals 32 for some group. `dec_src_block`: the 32 entries starting at (s * 8 + h) * 32 lie in s * 8 to (s + 1) * 8 - 1. `dec_hid_block`: the 32 entries starting at (s * 8 + h) * 32 lie in h * 32 to (h + 1) * 32 - 1; within these entries no pair (dec_src_block, dec_hid_block) repeats. `dec_count`: entry s * 8 + h counts the live slots of that group; it equals 32 for some group.
All inputs are finite; a program needn't handle non-finite values.
Results may differ from a plain program's by a relative error of at most 0.0003.
Values sent between devices are 32-bit elements; how exact they have to be, the bound alone decides.
A program may use at most 64 MiB of HBM per device.

v0:
```python
import jax
import jax.numpy as jnp
from jax import lax
from jax.sharding import Mesh
from jax.sharding import PartitionSpec as P

HID_BLK = 32
GROUP = 16
SRC = ("src_0", "src_1", "src_2")
HID = ("hid_0", "hid_1")
SRC_HID = ("src_0", "src_1", "src_2", "hid_0", "hid_1")


HIGH = lax.Precision.HIGHEST
EPSILON = 1e-06


def filled_up(lines, length):
    spare = -lines.shape[0] % length
    if not spare:
        return lines
    return jnp.concatenate([lines, jnp.zeros((spare, *lines.shape[1:]), lines.dtype)])


def joined_along(pieces, dim):
    pieces = jnp.moveaxis(pieces, 0, dim)
    shape = pieces.shape
    return pieces.reshape(*shape[:dim], shape[dim] * shape[dim + 1], *shape[dim + 2 :])


def from_everyone(x, axis):
    length = lax.axis_size(axis)
    return lax.all_to_all(jnp.broadcast_to(x[None], (length, *x.shape)), axis, 0, 0, tiled=True)


def gather_directly(x, axis, dim):
    return joined_along(from_everyone(x, axis), dim)


def cut_along(x, dim, length):
    shape = x.shape
    pieces = x.reshape(*shape[:dim], length, shape[dim] // length, *shape[dim + 1 :])
    return jnp.moveaxis(pieces, dim, 0)


def summed_on_arrival(x, axis, dim):
    length = lax.axis_size(axis)
    pieces = lax.all_to_all(cut_along(x, dim, length), axis, 0, 0, tiled=True)
    return jnp.sum(pieces, axis=0)


def sum_by_parts(x, axes):
    lines = x.reshape(-1, x.shape[-1])
    padded = filled_up(lines, lax.axis_size(axes))
    whole = gather_directly(summed_on_arrival(padded, axes, 0), axes, 0)
    return lax.slice_in_dim(whole, 0, len(lines)).reshape(x.shape)


def one_axis_at_a_time(x, axes):
    for axis in axes:
        x = lax.psum(x, axis)
    return x


def normalize(total, gain, batch, channels):
    nodes, features, width = total.shape
    grouped = total.reshape(nodes, batch, channels, width)
    mean_square = jnp.mean(grouped * grouped, axis=2, keepdims=True)
    scaled = grouped * gain[None, None, :, None] * lax.rsqrt(mean_square + EPSILON)
    return scaled.reshape(nodes, features, width)


def body(
    source_field,
    hidden_gain,
    enc_tiles,
    enc_src_block,
    enc_hid_block,
    enc_count,
    dec_tiles,
    dec_src_block,
    dec_hid_block,
    dec_count,
):
    src_blocks, batch, channels, width = source_field.shape
    features = batch * channels
    flat = source_field.reshape(src_blocks, features, width)
    src_first = lax.axis_index(SRC) * src_blocks
    hid_first = lax.axis_index(HID) * HID_BLK
    enc_sources = enc_src_block - src_first
    enc_targets = enc_hid_block - hid_first
    dec_targets = dec_src_block - src_first
    dec_sources = dec_hid_block - hid_first
    src_range = jnp.arange(src_blocks, dtype=jnp.int32)
    hid_range = jnp.arange(HID_BLK, dtype=jnp.int32)
    slot_range = jnp.arange(GROUP, dtype=jnp.int32)

    def encode_group(step, partial_value):
        start = step * GROUP
        tiles = lax.dynamic_slice_in_dim(enc_tiles, start, GROUP, 0)
        sources = lax.dynamic_slice_in_dim(enc_sources, start, GROUP, 0)
        targets = lax.dynamic_slice_in_dim(enc_targets, start, GROUP, 0)
        alive = (start + slot_range < enc_count[0])[:, None]
        select = (sources[:, None] == src_range[None, :]).astype(jnp.float32)
        placing = (alive & (targets[:, None] == hid_range[None, :])).astype(jnp.float32)
        blocks = jnp.einsum("ts,sfc->tfc", select, flat, precision=HIGH)
        product = jnp.einsum("tfr,trc->tfc", blocks, tiles, precision=HIGH)
        return partial_value + jnp.einsum("th,tfc->hfc", placing, product, precision=HIGH)

    enc_groups = (enc_count[0] + GROUP - 1) // GROUP
    partial_value = lax.fori_loop(
        0, enc_groups, encode_group, jnp.zeros((HID_BLK, features, width), jnp.float32)
    )
    hidden = normalize(sum_by_parts(partial_value, SRC), hidden_gain, batch, channels)

    def fetch(start):
        sources = lax.dynamic_slice_in_dim(dec_sources, start, GROUP, 0)
        select = (sources[:, None] == hid_range[None, :]).astype(jnp.float32)
        return jnp.einsum("th,hfc->tfc", select, hidden, precision=HIGH)

    def decode_group(step, partial_back):
        start = step * GROUP
        tiles = lax.dynamic_slice_in_dim(dec_tiles, start, GROUP, 0)
        targets = lax.dynamic_slice_in_dim(dec_targets, start, GROUP, 0)
        alive = (start + slot_range < dec_count[0])[:, None]
        blocks = fetch(start)
        product = jnp.einsum("tfr,trc->tfc", blocks, tiles, precision=HIGH)
        placing = (alive & (targets[:, None] == src_range[None, :])).astype(jnp.float32)
        return partial_back + jnp.einsum("ts,tfc->sfc", placing, product, precision=HIGH)

    dec_groups = (dec_count[0] + GROUP - 1) // GROUP
    partial_back = lax.fori_loop(
        0, dec_groups, decode_group, jnp.zeros((src_blocks, features, width), jnp.float32)
    )
    total_points = src_blocks * lax.axis_size(SRC) * batch * width
    share_back = summed_on_arrival(partial_back, HID, 0)
    own_rows = share_back.shape[0]
    mine = lax.dynamic_slice_in_dim(flat, lax.axis_index(HID) * own_rows, own_rows, 0)
    difference = share_back - mine
    squares = jnp.sum(
        (difference * difference).reshape(own_rows, batch, channels, width), axis=(0, 1, 3)
    )
    sums = one_axis_at_a_time(squares, SRC_HID)
    returned = gather_directly(share_back, HID, 0)
    channel_rms = jnp.sqrt(sums / total_points + EPSILON)
    return (returned.reshape(source_field.shape), channel_rms)


def solution(mesh):
    split = Mesh(mesh.devices.reshape(4, 2, 4, 4, 2), ("src_0", "src_1", "src_2", "hid_0", "hid_1"))
    in_specs = (
        P(SRC, None, None, None),
        P(),
        P(SRC_HID, None, None),
        P(SRC_HID),
        P(SRC_HID),
        P(SRC_HID),
        P(SRC_HID, None, None),
        P(SRC_HID),
        P(SRC_HID),
        P(SRC_HID),
    )
    out_specs = (P(SRC, None, None, None), P())
    return jax.shard_map(body, mesh=split, in_specs=in_specs, out_specs=out_specs, check_vma=False)
```

profile of v0, /device:TPU:1, one launch (start us, length us, event | category | flops | bytes accessed | tf_op | source)
XLA Modules:
  0.0 229.1 jit_solution(15872392379640564132)
XLA Ops:
  1.3 2.1 copy.57
  3.4 0.7 broadcast_subtract_fusion
  4.1 0.4 broadcast_in_dim.14
  4.5 17.4 %while.22 = (s32[]{:T(128)}, f32[32,196,128]{2,0,1:T(8,128)S(1)}, s32[]{:T(128)}, s32[1]{0:T(128)}, s32[32]{0:T(128)S(1)}, /*index=5*/s32[32]{0:T(128)S(1)}, f32...) while((s32[]{:T(128)}, f32[32,196,128]{2,0,1:T(8,128)S(1)}, ...), condition=%wide.region_1.2_spmd.clone, body=%wide.region_0.1_spmd.clone.sunk | while | flops 810042496 | bytes 23085684 | solution.py:111
  4.6 2.1 fusion.73
  6.7 3.2 %fusion.74 = f32[16,196,128]{2,1,0:T(8,128)S(1)} fusion(f32[16,196,128]{2,0,1:T(8,128)S(1)} %fusion.73, f32[32,128,128]{2,1,0:T(8,128)S(1)} %copy-done.1, s32[]{:T(128)S(6)} %select_n.28), kind=kOutput, calls=%fused_computation.7.clone.1 | convolution fusion | flops 616562688 | bytes 4259844 | tf_op jit(solution)/shard_map/while/body/tfr,trc->tfc/dot_general | solution.py:107
  10.0 0.7 fusion.75
  10.6 2.6 %convolution_add_fusion.2 = f32[32,196,128]{2,0,1:T(8,128)S(1)} fusion(f32[32,196,128]{2,0,1:T(8,128)S(1)} %get-tuple-element.337, f32[16,196,128]{2,1,0:T(8,128)S(1)} %fusion.74, s32[16]{0:T(128)S(1)} %dynamic_slice.41, pred[16]{0:T(512)(128)(4,1)S(1)} %fusion.75), kind=kOutput, calls=%fused_computation.6.clone.1 | convolution fusion | flops 154944512 | bytes 8028240 | tf_op jit(solution)/shard_map/while/body/th,tfc->hfc/dot_general | solution.py:108
  13.3 2.1 fusion.73
  15.4 3.2 %fusion.74 = f32[16,196,128]{2,1,0:T(8,128)S(1)} fusion(f32[16,196,128]{2,0,1:T(8,128)S(1)} %fusion.73, f32[32,128,128]{2,1,0:T(8,128)S(1)} %copy-done.1, s32[]{:T(128)S(6)} %select_n.28), kind=kOutput, calls=%fused_computation.7.clone.1 | convolution fusion | flops 616562688 | bytes 4259844 | tf_op jit(solution)/shard_map/while/body/tfr,trc->tfc/dot_general | solution.py:107
  18.7 0.7 fusion.75
  19.3 2.6 %convolution_add_fusion.2 = f32[32,196,128]{2,0,1:T(8,128)S(1)} fusion(f32[32,196,128]{2,0,1:T(8,128)S(1)} %get-tuple-element.337, f32[16,196,128]{2,1,0:T(8,128)S(1)} %fusion.74, s32[16]{0:T(128)S(1)} %dynamic_slice.41, pred[16]{0:T(512)(128)(4,1)S(1)} %fusion.75), kind=kOutput, calls=%fused_computation.6.clone.1 | convolution fusion | flops 154944512 | bytes 8028240 | tf_op jit(solution)/shard_map/while/body/th,tfc->hfc/dot_general | solution.py:108
  21.9 1.9 copy.58
  23.8 50.3 %all_to_all.20 = f32[32,196,128]{2,1,0:T(8,128)S(1)} all-to-all(f32[32,196,128]{2,1,0:T(8,128)S(1)} %copy.58), channel_id=1, replica_groups=mesh['src_0'=4,'src_1'=2,'src_2'=4,'hid_0'=4,'hid_1'=2] {'src_0','src_1'..., dimensions={0} | all-to-all | bytes 6422528 | tf_op jit(solution)/shard_map/all_to_all | solution.py:48
  74.1 0.2 reduce_sum.45
  74.2 1.9 broadcast_in_dim.15
  76.1 4.2 %all-to-all-start.1 = ((f32[32,196,128]{2,1,0:T(8,128)}), f32[32,196,128]{2,1,0:T(8,128)S(1)}, u32[]{:S(2)}, u32[]{:S(2)}) async-start(f32[32,196,128]{2,1,0:T(8,128)} %broadcast_in_dim.15), calls=%async_computation.1 | async-start | bytes 6553600 | tf_op jit(solution)/shard_map/all_to_all | solution.py:33
  81.1 43.3 %all-to-all-done.1 = f32[32,196,128]{2,1,0:T(8,128)S(1)} async-done(((f32[32,196,128]{2,1,0:T(8,128)}), f32[32,196,128]{2,1,0:T(8,128)S(1)}, u32[]{:S(2)}, u32[]{:S(2)}) %all-to-all-start.1) | async-done | bytes 3211296 | tf_op jit(solution)/shard_map/all_to_all | solution.py:33
  124.4 2.6 %copy_multiply_fusion = f32[32,196,128]{2,0,1:T(8,128)} fusion(f32[32,196,128]{2,1,0:T(8,128)S(1)} %all-to-all-done.1), kind=kLoop, calls=%fused_computation.42 | loop fusion | flops 802816 | bytes 6422528 | tf_op jit(solution)/shard_map/mul | solution.py:68
  127.0 0.1 copy-done
  127.1 2.1 reduce_sum.46
  129.3 2.6 %bitcast_multiply_fusion = f32[32,196,128]{2,0,1:T(8,128)S(1)} fusion(f32[32,196,128]{2,1,0:T(8,128)} %copy-done, f32[32,2,128]{2,0,1:T(8,128)S(1)} %add_rsqrt_fusion, f32[196]{0:T(256)S(1)} %mul.61), kind=kLoop, calls=%fused_computation.41 | loop fusion | flops 1605632 | bytes 6456080 | tf_op jit(solution)/shard_map/mul | solution.py:69
  131.9 0.9 broadcast_in_dim.13
  132.8 16.7 %while.23 = (s32[]{:T(128)}, f32[8,196,128]{2,0,1:T(8,128)}, s32[]{:T(128)}, s32[1]{0:T(128)}, s32[32]{0:T(128)S(1)}, /*index=5*/s32[32]{0:T(128)S(1)}, f32[32,1...) while((s32[]{:T(128)}, f32[8,196,128]{2,0,1:T(8,128)}, ...), condition=%wide.region_5.6_spmd.clone, body=%wide.region_4.5_spmd.clone.sunk | while | flops 809440000 | bytes 20677236 | solution.py:132
  132.9 1.2 fusion.82
  134.1 0.3 copy-done.2
  134.5 3.2 %fusion.83 = f32[16,196,128]{2,1,0:T(8,128)S(1)} fusion(f32[16,196,128]{2,0,1:T(8,128)S(1)} %fusion.82, f32[32,128,128]{2,1,0:T(8,128)S(1)} %copy-done.2, s32[]{:T(128)S(6)} %select_n.29), kind=kOutput, calls=%fused_computation.23.clone.1 | convolution fusion | flops 616562688 | bytes 4259844 | tf_op jit(solution)/shard_map/while/body/tfr,trc->tfc/dot_general | solution.py:127
  137.7 0.7 fusion.84
  138.4 2.8 %fusion.85 = f32[8,196,128]{2,0,1:T(8,128)} fusion(f32[8,196,128]{2,0,1:T(8,128)} %get-tuple-element.373, f32[16,196,128]{2,1,0:T(8,128)S(1)} %fusion.83, s32[16]{0:T(128)S(1)} %dynamic_slice.44, pred[16]{0:T(512)(128)(4,1)S(1)} %fusion.84), kind=kOutput, calls=%fused_computation.27.clone.1 | convolution fusion | flops 38736128 | bytes 3211344 | tf_op jit(solution)/shard_map/while/body/ts,tfc->sfc/dot_general | solution.py:129
  141.2 1.2 fusion.82
  142.5 0.3 copy-done.2
  142.8 3.2 %fusion.83 = f32[16,196,128]{2,1,0:T(8,128)S(1)} fusion(f32[16,196,128]{2,0,1:T(8,128)S(1)} %fusion.82, f32[32,128,128]{2,1,0:T(8,128)S(1)} %copy-done.2, s32[]{:T(128)S(6)} %select_n.29), kind=kOutput, calls=%fused_computation.23.clone.1 | convolution fusion | flops 616562688 | bytes 4259844 | tf_op jit(solution)/shard_map/while/body/tfr,trc->tfc/dot_general | solution.py:127
  146.1 0.7 fusion.84
  146.7 2.8 %fusion.85 = f32[8,196,128]{2,0,1:T(8,128)} fusion(f32[8,196,128]{2,0,1:T(8,128)} %get-tuple-element.373, f32[16,196,128]{2,1,0:T(8,128)S(1)} %fusion.83, s32[16]{0:T(128)S(1)} %dynamic_slice.44, pred[16]{0:T(512)(128)(4,1)S(1)} %fusion.84), kind=kOutput, calls=%fused_computation.27.clone.1 | convolution fusion | flops 38736128 | bytes 3211344 | tf_op jit(solution)/shard_map/while/body/ts,tfc->sfc/dot_general | solution.py:129
  149.5 2.0 copy.62
  151.5 28.7 %all_to_all.21 = f32[8,1,196,128]{3,1,2,0:T(1,128)S(1)} all-to-all(f32[8,1,196,128]{3,1,2,0:T(1,128)S(1)} %copy.62), channel_id=1, replica_groups=mesh['src_0'=4,'src_1'=2,'src_2'=4,'hid_0'=4,'hid_1'=2] {'hid_0','hid_1'}, dimensions={0} | all-to-all | bytes 1605632 | tf_op jit(solution)/shard_map/all_to_all | solution.py:48
  180.2 0.6 reduce_sum.47
  180.7 1.3 broadcast_in_dim.16
  182.0 4.0 %all-to-all-start.3 = ((f32[8,1,196,128]{3,1,2,0:T(1,128)}), f32[8,1,196,128]{3,1,2,0:T(1,128)S(1)}, u32[]{:S(2)}, u32[]{:S(2)}) async-start(f32[8,1,196,128]{3,1,2,0:T(1,128)} %broadcast_in_dim.16), calls=%async_computation.3 | async-start | bytes 1605632 | tf_op jit(solution)/shard_map/all_to_all | solution.py:33
  186.0 2.2 multiply_reduce_fusion
  188.2 0.1 reduce_sum.50
  188.3 6.6 %psum.35 = f32[98]{0:T(128)S(1)} all-reduce(f32[98]{0:T(128)S(1)} %reduce_sum.51), channel_id=1, replica_groups=mesh['src_0'=4,'src_1'=2,'src_2'=4,'hid_0'=4,'hid_1'=2] {'src_0'}, use_global_device_ids=true, to_apply=%region_9.10 | all-reduce | flops 98 | bytes 784 | tf_op jit(solution)/shard_map/psum | solution.py:61
  194.9 4.7 %psum.36 = f32[98]{0:T(128)S(1)} all-reduce(f32[98]{0:T(128)S(1)} %psum.35), channel_id=1, replica_groups=mesh['src_0'=4,'src_1'=2,'src_2'=4,'hid_0'=4,'hid_1'=2] {'src_1'}, use_global_device_ids=true, to_apply=%region_10.11 | all-reduce | flops 98 | bytes 784 | tf_op jit(solution)/shard_map/psum | solution.py:61
  199.6 8.3 %psum.37 = f32[98]{0:T(128)S(1)} all-reduce(f32[98]{0:T(128)S(1)} %psum.36), channel_id=1, replica_groups=mesh['src_0'=4,'src_1'=2,'src_2'=4,'hid_0'=4,'hid_1'=2] {'src_2'}, use_global_device_ids=true, to_apply=%region_11.12 | all-reduce | flops 98 | bytes 784 | tf_op jit(solution)/shard_map/psum | solution.py:61
  207.9 10.2 %psum.38 = f32[98]{0:T(128)S(1)} all-reduce(f32[98]{0:T(128)S(1)} %psum.37), channel_id=1, replica_groups=mesh['src_0'=4,'src_1'=2,'src_2'=4,'hid_0'=4,'hid_1'=2] {'hid_0'}, use_global_device_ids=true, to_apply=%region_12.13 | all-reduce | flops 98 | bytes 784 | tf_op jit(solution)/shard_map/psum | solution.py:61
  218.1 9.1 %psum.39 = f32[98]{0:T(128)S(1)} all-reduce(f32[98]{0:T(128)S(1)} %psum.38), channel_id=1, replica_groups=mesh['src_0'=4,'src_1'=2,'src_2'=4,'hid_0'=4,'hid_1'=2] {'hid_1'}, use_global_device_ids=true, to_apply=%region_13.14 | all-reduce | flops 98 | bytes 784 | tf_op jit(solution)/shard_map/psum | solution.py:61
  227.2 0.5 add_sqrt_fusion
  227.8 1.3 copy.64
  (28 shorter events, 0.8 us)
Async XLA Ops:
  4.5 2.2 copy-start.1
  13.2 2.2 copy-start.1
  76.1 4.9 %copy-start.5 = (f32[98]{0:T(128)S(1)}, f32[98]{0:T(128)}, u32[]{:S(2)}) copy-start(f32[98]{0:T(128)} %param.15) | copy-start | bytes 1180
  76.1 5.0 %copy-start.3 = (s32[32]{0:T(128)S(1)}, s32[32]{0:T(128)}, u32[]{:S(2)}) copy-start(s32[32]{0:T(128)} %param.22) | copy-start | bytes 388
  76.1 5.0 %copy-start.4 = (s32[32]{0:T(128)S(1)}, s32[32]{0:T(128)}, u32[]{:S(2)}) copy-start(s32[32]{0:T(128)} %param.21) | copy-start | bytes 388
  76.1 48.3 %all-to-all-start.1 = ((f32[32,196,128]{2,1,0:T(8,128)}), f32[32,196,128]{2,1,0:T(8,128)S(1)}, u32[]{:S(2)}, u32[]{:S(2)}) async-start(f32[32,196,128]{2,1,0:T(8,128)} %broadcast_in_dim.15), calls=%async_computation.1 | async-start | bytes 6553600 | tf_op jit(solution)/shard_map/all_to_all | solution.py:33
  124.4 2.7 %copy-start = (f32[32,196,128]{2,1,0:T(8,128)}, f32[32,196,128]{2,1,0:T(8,128)S(1)}, u32[]{:S(2)}) copy-start(f32[32,196,128]{2,1,0:T(8,128)S(1)} %all-to-all-done.1) | copy-start | bytes 9633796
  132.9 1.6 copy-start.2
  141.2 1.6 copy-start.2
  182.0 45.7 %all-to-all-start.3 = ((f32[8,1,196,128]{3,1,2,0:T(1,128)}), f32[8,1,196,128]{3,1,2,0:T(1,128)S(1)}, u32[]{:S(2)}, u32[]{:S(2)}) async-start(f32[8,1,196,128]{3,1,2,0:T(1,128)} %broadcast_in_dim.16), calls=%async_computation.3 | async-start | bytes 1605632 | tf_op jit(solution)/shard_map/all_to_all | solution.py:33
where the time goes:
time: 229 us
  blocking collectives  118 us (52%)
  waiting for transfers between devices  43.3 us (19%)
  matrix products  30 us (13%)
  other arithmetic  14 us (6%)
  local copies, waits for them, and re-layouts  13.4 us (6%)
  starting transfers between devices  8.18 us (4%)
    all_to_all x2, blocking collectives, summed_on_arrival(): pieces = lax.all_to_all(cut_along(x, dim, length), axis, 0, 0, tiled=True)  79 us
    all_to_all x2, waiting for transfers between devices, from_everyone(): lax.all_to_all(jnp.broadcast_to(x[None], (length, *x.shape)), axis, 0, 0,...  43.3 us
    psum x5, blocking collectives, one_axis_at_a_time(): x = lax.psum(x, axis)  38.9 us
    all_to_all x2, starting transfers between devices, from_everyone(): lax.all_to_all(jnp.broadcast_to(x[None], (length, *x.shape)), axis, 0, 0,...  8.18 us
    dot_general x2, matrix products, decode_group(): product = jnp.einsum('tfr,trc->tfc', blocks, tiles, precision=HIGH)  6.31 us
    dot_general x2, matrix products, encode_group(): product = jnp.einsum('tfr,trc->tfc', blocks, tiles, precision=HIGH)  6.31 us
    dot_general x2, matrix products, decode_group(): jnp.einsum('ts,tfc->sfc', placing, product, precision=HIGH)  5.57 us
    dot_general x2, matrix products, encode_group(): jnp.einsum('th,tfc->hfc', placing, product, precision=HIGH)  5.15 us
  transfers between devices with their start and end apart: 2, of which 1 were waited for; matrix products, arithmetic and copies ran while one was open for 1% of the time, Pallas kernels for 0%

commit v1 on v0

v1 whole, which is shorter than its diff:
```python
import jax
import jax.numpy as jnp
from jax import lax
from jax.experimental import pallas as pl
from jax.experimental.pallas import tpu as pltpu
from jax.sharding import Mesh
from jax.sharding import PartitionSpec as P

CH = 98
BATCH = 2
TILE = 128
SRC_BLK = 8
HID_BLK = 32
CAP = 32
TOTAL_POINTS = 256 * BATCH * TILE
EPSILON = 1e-06
AXES = ("src_0", "src_1", "src_2", "hid_0", "hid_1")
SRC = ("src_0", "src_1", "src_2")
SIZES = {"src_0": 4, "src_1": 2, "src_2": 4, "hid_0": 4, "hid_1": 2}
MESH = pl.DeviceIdType.MESH
TILE_DMAS = 4

X, Z, Y, ZH, CORE = AXES


def hidden_slot(block, batch):
    x, z, y = block >> 3, (block >> 2) & 1, block & 3
    if batch == 0:
        return x * 8 + y * 2 + z
    return y * 8 + x * 2 + z


def split_pair(value):
    high = value.astype(jnp.bfloat16)
    low = (value - high.astype(jnp.float32)).astype(jnp.bfloat16)
    return high, low


def stacked_tile(tile):
    high, low = split_pair(tile)
    row = jnp.concatenate([high, low], axis=1)
    return jnp.concatenate([row, row], axis=0)


def full_product(left, right):
    both = jnp.dot(left, right, preferred_element_type=jnp.float32)
    return both[:, :TILE] + both[:, TILE:]


def tile_copies(tiles, held, sems):
    part = CAP // TILE_DMAS
    return [
        pltpu.make_async_copy(
            tiles.at[pl.ds(i * part, part)], held.at[pl.ds(i * part, part)], sems.at[i]
        )
        for i in range(TILE_DMAS)
    ]


def encode_kernel(src_ref, hid_ref, count_ref, field, tiles, out, held, left, sems):
    copies = tile_copies(tiles, held, sems)
    for copy in copies:
        copy.start()
    for s in range(SRC_BLK):
        for b in range(BATCH):
            left[s, b] = jnp.concatenate(split_pair(field[s, b]), axis=1)
    for b in range(BATCH):

        @pl.loop(0, HID_BLK)
        def _(j):
            out[b, j] = jnp.zeros((CH, TILE), jnp.float32)

    for copy in copies:
        copy.wait()

    @pl.loop(0, count_ref[0])
    def _(k):
        s = src_ref[k] & (SRC_BLK - 1)
        t = hid_ref[k] & (HID_BLK - 1)
        right = stacked_tile(held[k])
        for b in range(BATCH):
            slot = hidden_slot(t, b)
            out[b, slot] = out[b, slot] + full_product(left[s, b], right)


def decode_kernel(src_ref, hid_ref, count_ref, hidden, tiles, out, held, sems):
    copies = tile_copies(tiles, held, sems)
    for copy in copies:
        copy.start()
    for s in range(SRC_BLK):
        for b in range(BATCH):
            out[s, b] = jnp.zeros((CH, TILE), jnp.float32)
    for copy in copies:
        copy.wait()

    @pl.loop(0, count_ref[0])
    def _(k):
        s = src_ref[k] & (SRC_BLK - 1)
        t = hid_ref[k] & (HID_BLK - 1)
        right = stacked_tile(held[k])
        for b in range(BATCH):
            left = jnp.concatenate(split_pair(hidden[b, hidden_slot(t, b)]), axis=1)
            out[s, b] = out[s, b] + full_product(left, right)


def shifted(axis, step):
    size = SIZES[axis]
    return lax.rem(lax.axis_index(axis) + (step + size), size)


class Sender:
    def __init__(self, send_sems, recv_sems):
        self.send_sems, self.recv_sems, self.count, self.sent = send_sems, recv_sems, 0, []

    def start(self, src, dst, where):
        i = self.count
        self.count += 1
        copy = pltpu.make_async_remote_copy(
            src_ref=src,
            dst_ref=dst,
            send_sem=self.send_sems.at[i],
            recv_sem=self.recv_sems.at[i],
            device_id=where,
            device_id_type=MESH,
        )
        copy.start()
        self.sent.append(copy)
        return copy

    def finish(self):
        for copy in self.sent:
            copy.wait_send()


def greet(peers):
    barrier = pltpu.get_barrier_semaphore()
    for peer in peers:
        pl.semaphore_signal(barrier, inc=1, device_id=peer, device_id_type=MESH)
    pl.semaphore_wait(barrier, len(peers))


class RingSum:
    def __init__(self, sender, axis, part, landed, total):
        self.s, self.axis, self.part, self.landed, self.total = sender, axis, part, landed, total

    def begin(self):
        s, axis, part, landed = self.s, self.axis, self.part, self.landed
        right, left = {axis: shifted(axis, 1)}, {axis: shifted(axis, -1)}
        opposite = shifted(axis, 2)
        self.r1 = s.start(part(opposite, 0), landed.at[0], right)
        self.l1 = s.start(part(opposite, 1), landed.at[1], left)
        self.r2 = s.start(part(right[axis], 1), landed.at[2], right)
        self.l2 = s.start(part(left[axis], 0), landed.at[3], left)

    def middle(self):
        s, axis, part, landed = self.s, self.axis, self.part, self.landed
        right, left = {axis: shifted(axis, 1)}, {axis: shifted(axis, -1)}
        self.r1.wait_recv()
        landed[0] = landed[0] + part(right[axis], 0)[...]
        self.r3 = s.start(landed.at[0], landed.at[4], right)
        self.l1.wait_recv()
        landed[1] = landed[1] + part(left[axis], 1)[...]
        self.l3 = s.start(landed.at[1], landed.at[5], left)

    def end(self):
        me = lax.axis_index(self.axis)
        self.r2.wait_recv()
        self.l2.wait_recv()
        landed, part = self.landed, self.part
        self.r3.wait_recv()
        self.total(0)[...] = (part(me, 0)[...] + landed[3]) + landed[4]
        self.l3.wait_recv()
        self.total(1)[...] = (part(me, 1)[...] + landed[2]) + landed[5]


class RingGather:
    def __init__(self, sender, axis, part):
        self.s, self.axis, self.part = sender, axis, part

    def begin(self):
        s, axis, part = self.s, self.axis, self.part
        me = lax.axis_index(axis)
        right, left = {axis: shifted(axis, 1)}, {axis: shifted(axis, -1)}
        self.r1 = s.start(part(me, 0), part(me, 0), right)
        self.l1 = s.start(part(me, 1), part(me, 1), left)
        self.r2 = s.start(part(me, 1), part(me, 1), right)
        self.l2 = s.start(part(me, 0), part(me, 0), left)

    def middle(self):
        s, axis, part = self.s, self.axis, self.part
        right, left = {axis: shifted(axis, 1)}, {axis: shifted(axis, -1)}
        self.r1.wait_recv()
        self.r3 = s.start(part(left[axis], 0), part(left[axis], 0), right)
        self.l1.wait_recv()
        self.l3 = s.start(part(right[axis], 1), part(right[axis], 1), left)

    def end(self):
        for copy in (self.r2, self.l2, self.r3, self.l3):
            copy.wait_recv()


def run_together(rings):
    for ring in rings:
        ring.begin()
    for ring in rings:
        ring.middle()
    for ring in rings:
        ring.end()


def hidden_kernel(
    partial, gain, out, first_in, first_sum, second_in, second_sum, last_in, send_sems, recv_sems
):
    greet(
        [{X: shifted(X, 1)}, {X: shifted(X, -1)}, {Y: shifted(Y, 1)}, {Y: shifted(Y, -1)}]
        + [{Z: shifted(Z, 1)}]
    )
    s = Sender(send_sems, recv_sems)
    colours = ((X, Y), (Y, X))
    z = lax.axis_index(Z)
    other = 1 - z

    def first_sums(b, axis):
        return RingSum(
            s,
            axis,
            lambda i, h: partial.at[b, pl.ds(i * 8 + h * 4, 4)],
            first_in.at[b],
            lambda h: first_sum.at[b, pl.ds(h * 4, 4)],
        )

    def second_sums(b, axis):
        return RingSum(
            s,
            axis,
            lambda i, h: first_sum.at[b, i * 2 + h],
            second_in.at[b],
            lambda h: second_sum.at[b, h],
        )

    run_together([first_sums(b, colours[b][0]) for b in range(BATCH)])
    run_together([second_sums(b, colours[b][1]) for b in range(BATCH)])
    swaps = [
        s.start(second_sum.at[b, other], last_in.at[b], {Z: other}) for b in range(BATCH)
    ]
    rows = lax.broadcasted_iota(jnp.int32, (CH, CH), 0)
    columns = lax.broadcasted_iota(jnp.int32, (CH, CH), 1)
    scale = jnp.sum(
        jnp.where(rows == columns, jnp.broadcast_to(gain[...], (CH, CH)), 0.0),
        axis=1,
        keepdims=True,
    )
    pairs = []
    for b in range(BATCH):
        p, q = (lax.axis_index(axis) for axis in colours[b])
        swaps[b].wait_recv()
        value = second_sum[b, z] + last_in[b]
        mean_square = jnp.sum(value * value, axis=0, keepdims=True) * (1.0 / CH)
        slot = out.at[b, p * 8 + q * 2 + z]
        slot[...] = value * scale * lax.rsqrt(mean_square + EPSILON)
        pairs.append(s.start(slot, slot, {Z: other}))
    for pair in pairs:
        pair.wait_recv()

    def second_gather(b, axis):
        p = lax.axis_index(colours[b][0])
        return RingGather(s, axis, lambda i, h: out.at[b, p * 8 + i * 2 + h])

    def first_gather(b, axis):
        return RingGather(s, axis, lambda i, h: out.at[b, pl.ds(i * 8 + h * 4, 4)])

    run_together([second_gather(b, colours[b][1]) for b in range(BATCH)])
    run_together([first_gather(b, colours[b][0]) for b in range(BATCH)])
    s.finish()


def returned_kernel(
    partial, field, out, rms, core_in, core_sum, ring_in, squares, square_in, send_sems, recv_sems
):
    core = lax.axis_index(CORE)
    twin = 1 - core
    zh = lax.axis_index(ZH)
    z = lax.axis_index(Z)
    column = [
        (dz, dh, dc) for dz in range(2) for dh in range(4) for dc in range(2) if (dz, dh, dc) != (0, 0, 0)
    ]

    def stack_peer(dz, dh, dc):
        return {Z: lax.rem(z + dz, 2), ZH: lax.rem(zh + dh, 4), CORE: lax.rem(core + dc, 2)}

    lines = [{X: shifted(X, i)} for i in (1, 2, 3)], [{Y: shifted(Y, i)} for i in (1, 2, 3)]
    greet(lines[0] + lines[1] + [stack_peer(*step) for step in column])
    s = Sender(send_sems, recv_sems)
    order = [lax.rem(zh + i, 4) for i in (2, 1, 3, 0)]
    crossing = [
        s.start(partial.at[twin * 4 + i], core_in.at[i], {CORE: twin}) for i in order
    ]
    for i, copy in zip(order, crossing):
        copy.wait_recv()
        core_sum[i] = partial[core * 4 + i] + core_in[i]
    mine = out.at[core * 4 + zh]
    ring = RingSum(s, ZH, lambda i, h: core_sum.at[i, h], ring_in, lambda h: mine.at[h])
    run_together([ring])
    gather = RingGather(s, ZH, lambda i, h: out.at[core * 4 + i, h])
    gather.begin()
    error = mine[...] - field[core * 4 + zh]
    error = error * error
    column_sum = jnp.sum(error[0] + error[1], axis=1, keepdims=True)
    rows = lax.broadcasted_iota(jnp.int32, (CH, TILE), 0)
    columns = lax.broadcasted_iota(jnp.int32, (CH, TILE), 1)
    line = jnp.sum(jnp.where(rows == columns, column_sum, 0.0), axis=0, keepdims=True)
    squares[0] = jnp.broadcast_to(line, (8, TILE))

    def exchange(stage, first, peers):
        copies = [
            s.start(squares.at[stage], square_in.at[first + i], peer)
            for i, peer in enumerate(peers)
        ]
        return copies

    def collect(stage, first, copies):
        total = squares[stage]
        for i, copy in enumerate(copies):
            copy.wait_recv()
            total = total + square_in[first + i]
        squares[stage + 1] = total

    copies = exchange(0, 0, lines[0])
    gather.middle()
    collect(0, 0, copies)
    copies = exchange(1, 3, lines[1])
    swaps = [s.start(mine, mine, {CORE: twin})]
    collect(1, 3, copies)
    copies = exchange(2, 6, [stack_peer(*step) for step in column])
    gather.end()
    for i in (1, 2, 3):
        block = out.at[core * 4 + lax.rem(zh + i, 4)]
        swaps.append(s.start(block, block, {CORE: twin}))
    collect(2, 6, copies)
    rms[...] = jnp.sqrt(squares[3] * (1.0 / TOTAL_POINTS) + EPSILON)
    for copy in swaps:
        copy.wait_recv()
    s.finish()


VMEM = pl.BlockSpec(memory_space=pltpu.VMEM)
SMEM = pl.BlockSpec(memory_space=pltpu.SMEM)
ANY = pl.BlockSpec(memory_space=pl.ANY)


def f32(*shape):
    return jax.ShapeDtypeStruct(shape, jnp.float32)


def body(
    source_field,
    hidden_gain,
    enc_tiles,
    enc_src_block,
    enc_hid_block,
    enc_count,
    dec_tiles,
    dec_src_block,
    dec_hid_block,
    dec_count,
):
    held = pltpu.VMEM((CAP, TILE, TILE), jnp.float32)
    block = (CH, TILE)
    partial = pl.pallas_call(
        encode_kernel,
        out_shape=f32(BATCH, HID_BLK, *block),
        in_specs=[SMEM, SMEM, SMEM, VMEM, ANY],
        out_specs=VMEM,
        scratch_shapes=[
            held,
            pltpu.VMEM((SRC_BLK, BATCH, CH, 2 * TILE), jnp.bfloat16),
            pltpu.SemaphoreType.DMA((TILE_DMAS,)),
        ],
    )(enc_src_block, enc_hid_block, enc_count, source_field, enc_tiles)
    hidden = pl.pallas_call(
        hidden_kernel,
        out_shape=f32(BATCH, HID_BLK, *block),
        in_specs=[VMEM, VMEM],
        out_specs=VMEM,
        scratch_shapes=[
            pltpu.VMEM((BATCH, 6, 4, *block), jnp.float32),
            pltpu.VMEM((BATCH, 8, *block), jnp.float32),
            pltpu.VMEM((BATCH, 6, *block), jnp.float32),
            pltpu.VMEM((BATCH, 2, *block), jnp.float32),
            pltpu.VMEM((BATCH, *block), jnp.float32),
            pltpu.SemaphoreType.DMA((52,)),
            pltpu.SemaphoreType.DMA((52,)),
        ],
        compiler_params=pltpu.CompilerParams(collective_id=0, has_side_effects=True),
    )(partial, hidden_gain.reshape(1, CH))
    partial_back = pl.pallas_call(
        decode_kernel,
        out_shape=f32(SRC_BLK, BATCH, *block),
        in_specs=[SMEM, SMEM, SMEM, VMEM, ANY],
        out_specs=VMEM,
        scratch_shapes=[held, pltpu.SemaphoreType.DMA((TILE_DMAS,))],
    )(dec_src_block, dec_hid_block, dec_count, hidden, dec_tiles)
    returned, rms = pl.pallas_call(
        returned_kernel,
        out_shape=(f32(SRC_BLK, BATCH, *block), f32(8, TILE)),
        in_specs=[VMEM, VMEM],
        out_specs=(VMEM, VMEM),
        scratch_shapes=[
            pltpu.VMEM((4, BATCH, *block), jnp.float32),
            pltpu.VMEM((4, BATCH, *block), jnp.float32),
            pltpu.VMEM((6, *block), jnp.float32),
            pltpu.VMEM((4, 8, TILE), jnp.float32),
            pltpu.VMEM((21, 8, TILE), jnp.float32),
            pltpu.SemaphoreType.DMA((41,)),
            pltpu.SemaphoreType.DMA((41,)),
        ],
        compiler_params=pltpu.CompilerParams(collective_id=1, has_side_effects=True),
    )(partial_back, source_field)
    return returned, rms[0, :CH]


def solution(mesh):
    split = Mesh(mesh.devices.reshape(4, 2, 4, 4, 2), AXES)
    every = P(AXES)
    in_specs = (
        P(SRC, None, None, None),
        P(),
        P(AXES, None, None),
        every,
        every,
        every,
        P(AXES, None, None),
        every,
        every,
        every,
    )
    out_specs = (P(SRC, None, None, None), P())
    return jax.shard_map(body, mesh=split, in_specs=in_specs, out_specs=out_specs, check_vma=False)
```

time: 229 us -> 122 us (0.53)
  blocking collectives: 118 us -> 0 us
  Pallas kernels: 0 us -> 114 us
  waiting for transfers between devices: 43.3 us -> 0 us
  matrix products: 30 us -> 0 us
  other arithmetic: 14 us -> 0 us
  starting transfers between devices: 8.18 us -> 0 us
  local copies, waits for them, and re-layouts: 13.4 us -> 5.76 us
    pallas_call x0 -> x4, Pallas kernels: none -> 114 us  [the longest x1 52.6 us: body(): pl.pallas_call(hidden_kernel, out_shape=f32(BATCH, HID_BLK, *block), in_s...]
    all_to_all x2 -> x0, blocking collectives: 79 us -> none  [summed_on_arrival(): pieces = lax.all_to_all(cut_along(x, dim, length), axis, 0, 0, tiled=True)]
    all_to_all x2 -> x0, waiting for transfers between devices: 43.3 us -> none  [from_everyone(): lax.all_to_all(jnp.broadcast_to(x[None], (length, *x.shape)), axis, 0, 0,...]
    psum x5 -> x0, blocking collectives: 38.9 us -> none  [one_axis_at_a_time(): x = lax.psum(x, axis)]
    dot_general x12 -> x0, matrix products: 30 us -> none  [the longest x2 6.31 us: decode_group(): product = jnp.einsum('tfr,trc->tfc', blocks, tiles, precision=HIGH)]
    all_to_all x2 -> x0, starting transfers between devices: 8.18 us -> none  [from_everyone(): lax.all_to_all(jnp.broadcast_to(x[None], (length, *x.shape)), axis, 0, 0,...]
    mul x2 -> x0, other arithmetic: 5.15 us -> none  [the longest x1 2.58 us: normalize(): grouped * gain[None, None, :, None] * lax.rsqrt(mean_square + EPSILON)]
    reduce_sum x5 -> x0, other arithmetic: 5.05 us -> none  [the longest x2 2.19 us: body(): jnp.sum((difference * difference).reshape(own_rows, batch, channels, widt...]
  transfers between devices with their start and end apart: 2 -> 0, of which waited for: 1 -> 0; matrix products, arithmetic and copies ran while one was open for 1% -> 0% of each run, Pallas kernels for 0% -> 0%
where the time goes in v1:
time: 122 us
  Pallas kernels  114 us (93%)
  local copies, waits for them, and re-layouts  5.76 us (5%)
  between operations  1.96 us (2%)
    pallas_call x1, Pallas kernels, body(): pl.pallas_call(hidden_kernel, out_shape=f32(BATCH, HID_BLK, *block), in_s...  52.6 us
    pallas_call x1, Pallas kernels, body(): pl.pallas_call(returned_kernel, out_shape=(f32(SRC_BLK, BATCH, *block), f...  43.6 us
    pallas_call x1, Pallas kernels, body(): pl.pallas_call(encode_kernel, out_shape=f32(BATCH, HID_BLK, *block), in_s...  10.1 us
    pallas_call x1, Pallas kernels, body(): pl.pallas_call(decode_kernel, out_shape=f32(SRC_BLK, BATCH, *block), in_s...  7.68 us
    unnamed x2, local copies, waits for them, and re-layouts  4.57 us

profile of v1, /device:TPU:1, one launch (start us, length us, event | category | flops | bytes accessed | tf_op | source)
XLA Modules:
  0.0 121.7 jit_solution(17118415455798527056)
XLA Ops:
  0.6 2.1 %copy.12.field = f32[8,2,98,128]{3,2,1,0:T(8,128)} copy(f32[8,2,98,128]{3,1,2,0:T(2,128)} %param.10) | data formatting | bytes 1605632 | tf_op args[0]
  3.4 10.1 %shard_map.113.partial = f32[2,32,98,128]{3,2,1,0:T(8,128)} custom-call(s32[32]{0:T(128)} %src_ref.2, s32[32]{0:T(128)} %hid_ref.2, s32[1]{0:T(128)S(6)} %copy.15.count_ref, f32[8,2,98,128]{3,2,1,0:T(8,128)} %copy.12.field, f32[32,128,128]{2,1,0:T(8,128)} %tiles.2), custom_call_target="tpu_custom_call" | custom-call | tf_op jit(solution)/shard_map/pallas_call | solution.py:369
  13.5 52.6 %shard_map.114.hidden = f32[2,32,98,128]{3,2,1,0:T(8,128)} custom-call(f32[2,32,98,128]{3,2,1,0:T(8,128)} %shard_map.113.partial, f32[1,98]{1,0:T(1,128)} %bitcast.3), custom_call_target="tpu_custom_call" | custom-call | tf_op jit(solution)/shard_map/pallas_call | solution.py:380
  66.8 7.7 %shard_map.115.partial = f32[8,2,98,128]{3,2,1,0:T(8,128)} custom-call(s32[32]{0:T(128)} %src_ref.3, s32[32]{0:T(128)} %hid_ref.3, s32[1]{0:T(128)S(6)} %copy.16.count_ref, f32[2,32,98,128]{3,2,1,0:T(8,128)} %shard_map.114.hidden, f32[32,128,128]{2,1,0:T(8,128)} %tiles.3), custom_call_target="tpu_custom_call" | custom-call | tf_op jit(solution)/shard_map/pallas_call | solution.py:396
  74.5 43.6 %shard_map.116 = (f32[8,2,98,128]{3,2,1,0:T(8,128)}, f32[8,128]{1,0:T(8,128)}) custom-call(f32[8,2,98,128]{3,2,1,0:T(8,128)} %shard_map.115.partial, f32[8,2,98,128]{3,2,1,0:T(8,128)} %copy.12.field), custom_call_target="tpu_custom_call" | custom-call | tf_op jit(solution)/shard_map/pallas_call | solution.py:403
  118.0 2.5 %copy.14 = f32[8,2,98,128]{3,1,2,0:T(2,128)} copy(f32[8,2,98,128]{3,2,1,0:T(8,128)} %get-tuple-element.6) | data formatting | bytes 1605632
  120.5 1.2 slice_bitcast_fusion

commit v2 on v0

v2 whole, which is shorter than its diff:
```python
import jax
import jax.numpy as jnp
from jax import lax
from jax.experimental import pallas as pl
from jax.experimental.pallas import tpu as pltpu
from jax.sharding import Mesh
from jax.sharding import PartitionSpec as P

CH = 98
BATCH = 2
TILE = 128
ROWS = CH * BATCH
SRC_BLK = 8
HID_BLK = 32
CAP = 32
NONE = CAP
TOTAL_POINTS = 256 * BATCH * TILE
EPSILON = 1e-06
AXES = ("src_0", "src_1", "src_2", "hid_0", "hid_1")
SRC = ("src_0", "src_1", "src_2")
SIZES = {"src_0": 4, "src_1": 2, "src_2": 4, "hid_0": 4, "hid_1": 2}
MESH = pl.DeviceIdType.MESH
TILE_DMAS = 4
UNROLL = 4
N_SEMS = 176

X, Z, Y, ZH, CORE = AXES
CUTS = ((0, 96), (96, 100))
COLOURS = ((X, Y), (Y, X))


def slot_of(block, colour):
    x, z, y = block >> 3, (block >> 2) & 1, block & 3
    if colour == 0:
        return x * 8 + y * 2 + z
    return y * 8 + x * 2 + z


def block_in(slot, colour):
    p, q, z = slot >> 3, (slot >> 1) & 3, slot & 1
    if colour == 0:
        return p * 8 + z * 4 + q
    return q * 8 + z * 4 + p


def split_pair(value):
    high = value.astype(jnp.bfloat16)
    low = (value - high.astype(jnp.float32)).astype(jnp.bfloat16)
    return jnp.concatenate([high, low], axis=1)


def stacked_tile(tile):
    row = split_pair(tile)
    return jnp.concatenate([row, row], axis=0)


def full_product(left, right):
    both = jnp.dot(left, right, preferred_element_type=jnp.float32)
    return both[:, :TILE] + both[:, TILE:]


def tile_copies(tiles, held, sems):
    part = CAP // TILE_DMAS
    return [
        pltpu.make_async_copy(
            tiles.at[pl.ds(i * part, part)], held.at[pl.ds(i * part, part)], sems.at[i]
        )
        for i in range(TILE_DMAS)
    ]


def shifted(axis, step):
    size = SIZES[axis]
    return lax.rem(lax.axis_index(axis) + (step + size), size)


def chain(targets, count):
    row = lax.broadcasted_iota(jnp.int32, (CAP, CAP), 0)
    lane = lax.broadcasted_iota(jnp.int32, (CAP, CAP), 1)
    along = jnp.broadcast_to(targets, (CAP, CAP))
    down = jnp.sum(jnp.where(row == lane, along, 0), axis=1, keepdims=True)
    live = lane < count
    before = jnp.max(jnp.where(live & (lane < row) & (along == down), lane, -1), axis=1, keepdims=True)
    last = jnp.max(jnp.where(live & (along == row), lane, -1), axis=1, keepdims=True)
    return jnp.where(before < 0, NONE, before), jnp.where(last < 0, NONE, last)


class Sender:
    def __init__(self, send_sems, recv_sems):
        self.send_sems, self.recv_sems, self.count, self.sent = send_sems, recv_sems, 0, []

    def start(self, src, dst, where):
        i = self.count
        self.count += 1
        copy = pltpu.make_async_remote_copy(
            src_ref=src,
            dst_ref=dst,
            send_sem=self.send_sems.at[i],
            recv_sem=self.recv_sems.at[i],
            device_id=where,
            device_id_type=MESH,
        )
        copy.start()
        self.sent.append(copy)
        return copy

    def finish(self):
        for copy in self.sent:
            copy.wait_send()


class RingSum:
    def __init__(self, sender, axis, part, landed, total):
        self.s, self.axis, self.part, self.landed, self.total = sender, axis, part, landed, total
        self.right, self.left = {axis: shifted(axis, 1)}, {axis: shifted(axis, -1)}

    def begin_far(self):
        opposite = shifted(self.axis, 2)
        self.r1 = self.s.start(self.part(opposite, 0), self.landed(0), self.right)
        self.l1 = self.s.start(self.part(opposite, 1), self.landed(1), self.left)

    def begin_right(self):
        self.r2 = self.s.start(self.part(self.right[self.axis], 1), self.landed(2), self.right)

    def begin_left(self):
        self.l2 = self.s.start(self.part(self.left[self.axis], 0), self.landed(3), self.left)

    def begin(self):
        self.begin_far()
        self.begin_right()
        self.begin_left()

    def middle_right(self):
        self.r1.wait_recv()
        self.landed(0)[...] = self.landed(0)[...] + self.part(self.right[self.axis], 0)[...]
        self.r3 = self.s.start(self.landed(0), self.landed(4), self.right)

    def middle_left(self):
        self.l1.wait_recv()
        self.landed(1)[...] = self.landed(1)[...] + self.part(self.left[self.axis], 1)[...]
        self.l3 = self.s.start(self.landed(1), self.landed(5), self.left)

    def middle(self):
        self.middle_right()
        self.middle_left()

    def end(self):
        me = lax.axis_index(self.axis)
        landed, part = self.landed, self.part
        self.r2.wait_recv()
        self.l2.wait_recv()
        self.r3.wait_recv()
        self.total(0)[...] = (part(me, 0)[...] + landed(3)[...]) + landed(4)[...]
        self.l3.wait_recv()
        self.total(1)[...] = (part(me, 1)[...] + landed(2)[...]) + landed(5)[...]


class RingGather:
    def __init__(self, sender, axis, part):
        self.s, self.axis, self.part = sender, axis, part
        self.me = lax.axis_index(axis)
        self.right, self.left = {axis: shifted(axis, 1)}, {axis: shifted(axis, -1)}
        self.rights, self.lefts = [], []

    def give(self, half):
        mine = self.part(self.me, half)
        self.rights.append(self.s.start(mine, mine, self.right))
        self.lefts.append(self.s.start(mine, mine, self.left))


def whole_kernel(
    enc_src,
    enc_hid,
    enc_count,
    dec_src,
    dec_hid,
    dec_count,
    field,
    gain,
    enc_tiles,
    dec_tiles,
    out,
    rms,
    enc_held,
    dec_held,
    table,
    table_s,
    blocks,
    left,
    right,
    sums,
    partial_0,
    partial_1,
    first_in_0,
    first_in_1,
    first_sum_0,
    first_sum_1,
    second_in_0,
    second_in_1,
    second_sum_0,
    second_sum_1,
    last_in_0,
    last_in_1,
    hidden_0,
    hidden_1,
    back_0,
    back_1,
    core_in_0,
    core_in_1,
    core_sum_0,
    core_sum_1,
    ring_in_0,
    ring_in_1,
    result_0,
    result_1,
    squares,
    square_in,
    local_sems,
    send_sems,
    recv_sems,
):
    partial = (partial_0, partial_1)
    first_in, first_sum = (first_in_0, first_in_1), (first_sum_0, first_sum_1)
    second_in, second_sum = (second_in_0, second_in_1), (second_sum_0, second_sum_1)
    last_in, hidden = (last_in_0, last_in_1), (hidden_0, hidden_1)
    back, core_in, core_sum = (back_0, back_1), (core_in_0, core_in_1), (core_sum_0, core_sum_1)
    ring_in, result = (ring_in_0, ring_in_1), (result_0, result_1)
    both = (0, 1)
    x, y, z = lax.axis_index(X), lax.axis_index(Y), lax.axis_index(Z)
    zh, core = lax.axis_index(ZH), lax.axis_index(CORE)
    other, twin = 1 - z, 1 - core
    where = {X: x, Y: y}

    lines = [[{axis: shifted(axis, i)} for i in (1, 2, 3)] for axis in (X, Y)]
    stack = [
        {Z: lax.rem(z + dz, 2), ZH: lax.rem(zh + dh, 4), CORE: lax.rem(core + dc, 2)}
        for dz in range(2)
        for dh in range(4)
        for dc in range(2)
        if dz + dh + dc
    ]
    peers = lines[0] + lines[1] + stack
    barrier = pltpu.get_barrier_semaphore()
    for peer in peers:
        pl.semaphore_signal(barrier, inc=1, device_id=peer, device_id_type=MESH)

    enc_copies = tile_copies(enc_tiles, enc_held, local_sems.at[0])
    dec_copies = tile_copies(dec_tiles, dec_held, local_sems.at[1])
    for copy in enc_copies:
        copy.start()

    before, last = chain(enc_hid[...] & (HID_BLK - 1), enc_count[0])
    before_back, last_back = chain(dec_src[...] & (SRC_BLK - 1), dec_count[0])
    lane = lax.broadcasted_iota(jnp.int32, (CAP, TILE), 1)
    table[...] = jnp.where(
        lane == 0, before, jnp.where(lane == 1, last, jnp.where(lane == 2, before_back, last_back))
    )
    sums[NONE] = jnp.zeros((ROWS, TILE), jnp.float32)
    for s in range(SRC_BLK):
        value = field[s * ROWS : (s + 1) * ROWS]
        blocks[s] = value
        left[s] = split_pair(value)
    table_copy = pltpu.make_async_copy(table, table_s, local_sems.at[2, 0])
    table_copy.start()
    for copy in dec_copies:
        copy.start()
    table_copy.wait()
    for copy in enc_copies:
        copy.wait()

    @pl.loop(0, CAP // UNROLL)
    def _(step):
        for i in range(UNROLL):
            k = step * UNROLL + i
            product = full_product(left[enc_src[k] & (SRC_BLK - 1)], stacked_tile(enc_held[k]))
            sums[k] = sums[table_s[k, 0]] + product

    @pl.loop(0, HID_BLK)
    def _(slot):
        for c in both:
            start, rows = CUTS[c]
            partial[c][slot] = sums[table_s[block_in(slot, c), 1], start : start + rows]

    pl.semaphore_wait(barrier, len(peers))
    s = Sender(send_sems, recv_sems)

    order = (2, 1, 3, 0)

    def first_ring(c, i):
        p, q = COLOURS[c]
        there = shifted(q, order[i])
        return RingSum(
            s,
            p,
            lambda m, h: partial[c].at[m * 8 + there * 2 + h],
            lambda n: first_in[c].at[i, n],
            lambda h: first_sum[c].at[there * 2 + h],
        )

    first = [[first_ring(c, i) for i in range(4)] for c in both]
    second = [
        RingSum(
            s,
            COLOURS[c][1],
            lambda m, h, c=c: first_sum[c].at[m * 2 + h],
            lambda n, c=c: second_in[c].at[n],
            lambda h, c=c: second_sum[c].at[h],
        )
        for c in both
    ]
    for i in (0, 1):
        for c in both:
            first[c][i].begin()
    for copy in dec_copies:
        copy.wait()

    @pl.loop(0, CAP)
    def _(k):
        right[k] = stacked_tile(dec_held[k])

    def feed(c, i):
        ring = second[c]
        if i == 0:
            ring.begin_far()
        elif i == 1:
            ring.begin_right()
            ring.middle_right()
        elif i == 2:
            ring.begin_left()
            ring.middle_left()

    for i in range(4):
        for c in both:
            first[c][i].middle()
            if i + 2 < 4:
                first[c][i + 2].begin()
        if i >= 1:
            for c in both:
                first[c][i - 1].end()
                feed(c, i - 1)
    swaps = []
    for c in both:
        first[c][3].end()
        second[c].end()
        swaps.append(s.start(second_sum[c].at[other], last_in[c], {Z: other}))

    row = lax.broadcasted_iota(jnp.int32, (ROWS, CH), 0)
    column = lax.broadcasted_iota(jnp.int32, (ROWS, CH), 1)
    scale = jnp.sum(
        jnp.where((row >> 1) == column, jnp.broadcast_to(gain[...], (ROWS, CH)), 0.0),
        axis=1,
        keepdims=True,
    )
    values, evens, odds = [], [], []
    for c in both:
        swaps[c].wait_recv()
        value = second_sum[c][z] + last_in[c][...]
        values.append(value)
        parity = lax.broadcasted_iota(jnp.int32, value.shape, 0) & 1
        square = value * value
        evens.append(jnp.sum(jnp.where(parity == 0, square, 0.0), axis=0, keepdims=True))
        odds.append(jnp.sum(jnp.where(parity == 1, square, 0.0), axis=0, keepdims=True))
    even = lax.rsqrt((evens[0] + evens[1]) * (1.0 / CH) + EPSILON)
    odd = lax.rsqrt((odds[0] + odds[1]) * (1.0 / CH) + EPSILON)
    for c in both:
        start, rows = CUTS[c]
        parity = lax.broadcasted_iota(jnp.int32, (rows, TILE), 0) & 1
        p, q = (where[axis] for axis in COLOURS[c])
        hidden[c][p * 8 + q * 2 + z] = (
            values[c] * scale[start : start + rows] * jnp.where(parity == 0, even, odd)
        )

    def first_gather(c, step):
        p, q = COLOURS[c]
        there = shifted(q, step)
        return RingGather(s, p, lambda m, h: hidden[c].at[m * 8 + there * 2 + h])

    def second_gather(c):
        p, q = COLOURS[c]
        return RingGather(s, q, lambda m, h: hidden[c].at[where[p] * 8 + m * 2 + h])

    outer = [[first_gather(c, step) for step in (0, 3, 1, 2)] for c in both]
    inner = [second_gather(c) for c in both]
    pairs = []
    for c in both:
        mine = inner[c].part(inner[c].me, z)
        pairs.append(s.start(mine, mine, {Z: other}))
        inner[c].give(z)
    for c in both:
        outer[c][0].give(z)
    for c in both:
        pairs[c].wait_recv()
        inner[c].give(other)
    for c in both:
        outer[c][0].give(other)

    def arrive(ring):
        for copy in ring.rights + ring.lefts:
            copy.wait_recv()

    def forward(ring):
        far_right, far_left = ring.part(ring.left[ring.axis], 0), ring.part(ring.right[ring.axis], 1)
        ring.last = [s.start(far_right, far_right, ring.right), s.start(far_left, far_left, ring.left)]

    for c in both:
        arrive(inner[c])
        forward(inner[c])
        for ring in outer[c][1:3]:
            ring.give(0)
            ring.give(1)
    for c in both:
        arrive(outer[c][0])
        forward(outer[c][0])
    for c in both:
        for copy in inner[c].last:
            copy.wait_recv()
        outer[c][3].give(0)
        outer[c][3].give(1)
    for n in (1, 2, 3):
        for c in both:
            arrive(outer[c][n])
            forward(outer[c][n])
    for n in range(4):
        for c in both:
            for copy in outer[c][n].last:
                copy.wait_recv()

    @pl.loop(0, CAP // UNROLL)
    def _(step):
        for i in range(UNROLL):
            k = step * UNROLL + i
            block = dec_hid[k] & (HID_BLK - 1)
            pieces = [split_pair(hidden[c][slot_of(block, c)]) for c in both]
            product = full_product(jnp.concatenate(pieces, axis=0), right[k])
            sums[k] = sums[table_s[k, 2]] + product

    @pl.loop(0, SRC_BLK)
    def _(i):
        for c in both:
            start, rows = CUTS[c]
            back[c][i] = sums[table_s[i, 3], start : start + rows]

    crossing = {}
    for step in order:
        m = lax.rem(zh + step, 4)
        for c in both:
            crossing[step, c] = s.start(
                back[c].at[twin * 4 + m], core_in[c].at[m], {CORE: twin}
            )
    for step in order:
        m = lax.rem(zh + step, 4)
        for c in both:
            crossing[step, c].wait_recv()
            core_sum[c][m] = back[c][core * 4 + m] + core_in[c][m]
    column_ring = RingSum(
        s,
        ZH,
        lambda m, h: core_sum[h].at[m],
        lambda n: ring_in[(0, 1, 1, 0, 0, 1)[n]].at[(0, 0, 1, 1, 2, 2)[n]],
        lambda h: result[h].at[core * 4 + zh],
    )
    column_ring.begin()
    column_ring.middle()
    column_ring.end()

    gather = RingGather(s, ZH, lambda m, h: result[h].at[core * 4 + m])
    gather.give(0)
    gather.give(1)
    total = None
    for c in both:
        start, rows = CUTS[c]
        error = result[c][core * 4 + zh] - blocks[core * 4 + zh, start : start + rows]
        by_row = jnp.sum(error * error, axis=1, keepdims=True)
        row = start + lax.broadcasted_iota(jnp.int32, (rows, TILE), 0)
        column = lax.broadcasted_iota(jnp.int32, (rows, TILE), 1)
        part = jnp.sum(jnp.where((row >> 1) == column, by_row, 0.0), axis=0, keepdims=True)
        total = part if total is None else total + part
    squares[0] = jnp.broadcast_to(total, (8, TILE))

    def to_twin(m, c):
        block = result[c].at[core * 4 + m]
        return s.start(block, block, {CORE: twin})

    twins = [to_twin(zh, c) for c in both]

    def exchange(stage, first_slot, those):
        return [
            s.start(squares.at[stage], square_in.at[first_slot + i], peer)
            for i, peer in enumerate(those)
        ]

    def collect(stage, first_slot, copies):
        value = squares[stage]
        for i, copy in enumerate(copies):
            copy.wait_recv()
            value = value + square_in[first_slot + i]
        squares[stage + 1] = value

    copies = exchange(0, 0, lines[0])
    arrive(gather)
    forward(gather)
    collect(0, 0, copies)
    copies = exchange(1, 3, lines[1])
    for step in (1, 3):
        for c in both:
            twins.append(to_twin(lax.rem(zh + step, 4), c))
    collect(1, 3, copies)
    copies = exchange(2, 6, stack)
    for c, copy in zip(both, gather.last):
        copy.wait_recv()
        twins.append(to_twin(lax.rem(zh + 2, 4), c))
    collect(2, 6, copies)
    rms[...] = jnp.sqrt(squares[3] * (1.0 / TOTAL_POINTS) + EPSILON)
    for copy in twins:
        copy.wait_recv()
    for i in range(SRC_BLK):
        for c in both:
            start, rows = CUTS[c]
            out[i * ROWS + start : i * ROWS + start + rows] = result[c][i]
    s.finish()


VMEM = pl.BlockSpec(memory_space=pltpu.VMEM)
SMEM = pl.BlockSpec(memory_space=pltpu.SMEM)
ANY = pl.BlockSpec(memory_space=pl.ANY)


def coloured(*lead):
    return [pltpu.VMEM((*lead, rows, TILE), jnp.float32) for _, rows in CUTS]


def body(
    source_field,
    hidden_gain,
    enc_tiles,
    enc_src_block,
    enc_hid_block,
    enc_count,
    dec_tiles,
    dec_src_block,
    dec_hid_block,
    dec_count,
):
    rows = source_field.transpose(0, 2, 1, 3).reshape(SRC_BLK * ROWS, TILE)
    held = pltpu.VMEM((CAP, TILE, TILE), jnp.float32)
    returned, rms = pl.pallas_call(
        whole_kernel,
        out_shape=(
            jax.ShapeDtypeStruct((SRC_BLK * ROWS, TILE), jnp.float32),
            jax.ShapeDtypeStruct((8, TILE), jnp.float32),
        ),
        in_specs=[SMEM, VMEM, SMEM, VMEM, SMEM, SMEM, VMEM, VMEM, ANY, ANY],
        out_specs=(VMEM, VMEM),
        scratch_shapes=[
            held,
            held,
            pltpu.VMEM((CAP, TILE), jnp.int32),
            pltpu.SMEM((CAP, TILE), jnp.int32),
            pltpu.VMEM((SRC_BLK, ROWS, TILE), jnp.float32),
            pltpu.VMEM((SRC_BLK, ROWS, 2 * TILE), jnp.bfloat16),
            pltpu.VMEM((CAP, 2 * TILE, 2 * TILE), jnp.bfloat16),
            pltpu.VMEM((CAP + 1, ROWS, TILE), jnp.float32),
            *coloured(HID_BLK),
            *coloured(4, 6),
            *coloured(8),
            *coloured(6),
            *coloured(2),
            *coloured(),
            *coloured(HID_BLK),
            *coloured(SRC_BLK),
            *coloured(4),
            *coloured(4),
            *coloured(3),
            *coloured(SRC_BLK),
            pltpu.VMEM((4, 8, TILE), jnp.float32),
            pltpu.VMEM((21, 8, TILE), jnp.float32),
            pltpu.SemaphoreType.DMA((3, TILE_DMAS)),
            pltpu.SemaphoreType.DMA((N_SEMS,)),
            pltpu.SemaphoreType.DMA((N_SEMS,)),
        ],
        compiler_params=pltpu.CompilerParams(collective_id=0, has_side_effects=True),
    )(
        enc_src_block,
        enc_hid_block.reshape(1, CAP),
        enc_count,
        dec_src_block.reshape(1, CAP),
        dec_hid_block,
        dec_count,
        rows,
        hidden_gain.reshape(1, CH),
        enc_tiles,
        dec_tiles,
    )
    returned = returned.reshape(SRC_BLK, CH, BATCH, TILE).transpose(0, 2, 1, 3)
    return returned, rms[0, :CH]


def solution(mesh):
    split = Mesh(mesh.devices.reshape(4, 2, 4, 4, 2), AXES)
    every = P(AXES)
    in_specs = (
        P(SRC, None, None, None),
        P(),
        P(AXES, None, None),
        every,
        every,
        every,
        P(AXES, None, None),
        every,
        every,
        every,
    )
    out_specs = (P(SRC, None, None, None), P())
    return jax.shard_map(body, mesh=split, in_specs=in_specs, out_specs=out_specs, check_vma=False)
```

time: 229 us -> 98.3 us (0.43)
  blocking collectives: 118 us -> 0 us
  Pallas kernels: 0 us -> 92.5 us
  waiting for transfers between devices: 43.3 us -> 0 us
  matrix products: 30 us -> 0 us
  other arithmetic: 14 us -> 0 us
  local copies, waits for them, and re-layouts: 13.4 us -> 3.26 us
  starting transfers between devices: 8.18 us -> 0 us
    pallas_call x0 -> x1, Pallas kernels: none -> 92.5 us  [body(): pl.pallas_call(whole_kernel, out_shape=(jax.ShapeDtypeStruct((SRC_BLK * R...]
    all_to_all x2 -> x0, blocking collectives: 79 us -> none  [summed_on_arrival(): pieces = lax.all_to_all(cut_along(x, dim, length), axis, 0, 0, tiled=True)]
    all_to_all x2 -> x0, waiting for transfers between devices: 43.3 us -> none  [from_everyone(): lax.all_to_all(jnp.broadcast_to(x[None], (length, *x.shape)), axis, 0, 0,...]
    psum x5 -> x0, blocking collectives: 38.9 us -> none  [one_axis_at_a_time(): x = lax.psum(x, axis)]
    dot_general x12 -> x0, matrix products: 30 us -> none  [the longest x2 6.31 us: decode_group(): product = jnp.einsum('tfr,trc->tfc', blocks, tiles, precision=HIGH)]
    all_to_all x2 -> x0, starting transfers between devices: 8.18 us -> none  [from_everyone(): lax.all_to_all(jnp.broadcast_to(x[None], (length, *x.shape)), axis, 0, 0,...]
    mul x2 -> x0, other arithmetic: 5.15 us -> none  [the longest x1 2.58 us: normalize(): grouped * gain[None, None, :, None] * lax.rsqrt(mean_square + EPSILON)]
    reduce_sum x5 -> x0, other arithmetic: 5.05 us -> none  [the longest x2 2.19 us: body(): jnp.sum((difference * difference).reshape(own_rows, batch, channels, widt...]
  transfers between devices with their start and end apart: 2 -> 0, of which waited for: 1 -> 0; matrix products, arithmetic and copies ran while one was open for 1% -> 0% of each run, Pallas kernels for 0% -> 0%
where the time goes in v2:
time: 98.3 us; the launch traced here: 97.7 us
  Pallas kernels  92.5 us (94%)
  local copies, waits for them, and re-layouts  3.26 us (3%)
  between operations  1.93 us (2%)
    pallas_call x1, Pallas kernels, body(): pl.pallas_call(whole_kernel, out_shape=(jax.ShapeDtypeStruct((SRC_BLK * R...  92.5 us
    unnamed x1, local copies, waits for them, and re-layouts  2.08 us

profile of v2, /device:TPU:1, one launch (start us, length us, event | category | flops | bytes accessed | tf_op | source)
XLA Modules:
  0.0 97.7 jit_solution(3506231704533007497)
XLA Ops:
  1.9 92.5 %shard_map.113 = (f32[1568,128]{1,0:T(8,128)}, f32[8,128]{1,0:T(8,128)}) custom-call(s32[32]{0:T(128)} %enc_src.1, s32[1,32]{1,0:T(1,128)} %bitcast.13, s32[1]{0:T(128)S(6)} %copy.13.enc_count, s32[1,32]{1,0:T(1,128)} %bitcast.14, s32[32]{0:T(128)} %dec_hid.1, s32[1]{0:T(128)S(6)} %copy.14.dec_count, f32[1568,128]{1,0:T(8,128)} %bitcast.12, ...), custom_call_target="tpu_custom_call" | custom-call | tf_op jit(solution)/shard_map/pallas_call | solution.py:546
  94.4 1.2 %slice_bitcast_fusion = f32[98]{0:T(128)} fusion(f32[8,128]{1,0:T(8,128)} %get-tuple-element.5), kind=kLoop, calls=%fused_computation | loop fusion | bytes 784 | tf_op jit(solution)/shard_map/squeeze | solution.py:595
  95.6 2.1 %copy.15 = f32[8,2,98,128]{3,1,2,0:T(2,128)} copy(f32[8,2,98,128]{3,1,2,0:T(2,128)} %bitcast.11) | data formatting | bytes 1605632

commit v3 on v2

--- a/solution.py
+++ b/solution.py
@@ -22,7 +22,8 @@
 MESH = pl.DeviceIdType.MESH
 TILE_DMAS = 4
 UNROLL = 4
-N_SEMS = 176
+N_SEMS = 184
+HALF = 48
 
 X, Z, Y, ZH, CORE = AXES
 CUTS = ((0, 96), (96, 100))
@@ -79,7 +80,7 @@
     lane = lax.broadcasted_iota(jnp.int32, (CAP, CAP), 1)
     along = jnp.broadcast_to(targets, (CAP, CAP))
     down = jnp.sum(jnp.where(row == lane, along, 0), axis=1, keepdims=True)
-    live = lane < count
+    live = lane < jnp.broadcast_to(count, (CAP, CAP))
     before = jnp.max(jnp.where(live & (lane < row) & (along == down), lane, -1), axis=1, keepdims=True)
     last = jnp.max(jnp.where(live & (along == row), lane, -1), axis=1, keepdims=True)
     return jnp.where(before < 0, NONE, before), jnp.where(last < 0, NONE, last)
@@ -169,18 +170,25 @@
 
 
 def whole_kernel(
+    enc_src_any,
+    enc_hid_any,
+    counts_any,
+    dec_src_any,
+    dec_hid_any,
+    field_any,
+    gain_any,
+    enc_tiles,
+    dec_tiles,
+    result_0,
+    result_1,
+    rms,
     enc_src,
     enc_hid,
-    enc_count,
+    counts,
     dec_src,
     dec_hid,
-    dec_count,
     field,
     gain,
-    enc_tiles,
-    dec_tiles,
-    out,
-    rms,
     enc_held,
     dec_held,
     table,
@@ -195,12 +203,14 @@
     first_in_1,
     first_sum_0,
     first_sum_1,
+    pair_in_0,
+    pair_in_1,
+    pair_sum_0,
+    pair_sum_1,
     second_in_0,
     second_in_1,
     second_sum_0,
     second_sum_1,
-    last_in_0,
-    last_in_1,
     hidden_0,
     hidden_1,
     back_0,
@@ -211,8 +221,6 @@
     core_sum_1,
     ring_in_0,
     ring_in_1,
-    result_0,
-    result_1,
     squares,
     square_in,
     local_sems,
@@ -221,8 +229,9 @@
 ):
     partial = (partial_0, partial_1)
     first_in, first_sum = (first_in_0, first_in_1), (first_sum_0, first_sum_1)
+    pair_in, pair_sum = (pair_in_0, pair_in_1), (pair_sum_0, pair_sum_1)
     second_in, second_sum = (second_in_0, second_in_1), (second_sum_0, second_sum_1)
-    last_in, hidden = (last_in_0, last_in_1), (hidden_0, hidden_1)
+    hidden = (hidden_0, hidden_1)
     back, core_in, core_sum = (back_0, back_1), (core_in_0, core_in_1), (core_sum_0, core_sum_1)
     ring_in, result = (ring_in_0, ring_in_1), (result_0, result_1)
     both = (0, 1)
@@ -241,39 +250,56 @@
     ]
     peers = lines[0] + lines[1] + stack
     barrier = pltpu.get_barrier_semaphore()
+    small = [
+        pltpu.make_async_copy(there, here, local_sems.at[2, i])
+        for i, (there, here) in enumerate(
+            (
+                (enc_src_any, enc_src),
+                (enc_hid_any, enc_hid),
+                (counts_any, counts),
+                (dec_src_any, dec_src),
+                (dec_hid_any, dec_hid),
+                (gain_any, gain),
+            )
+        )
+    ]
+    field_copy = pltpu.make_async_copy(field_any, field, local_sems.at[2, 7])
+    enc_copies = tile_copies(enc_tiles, enc_held, local_sems.at[0])
+    dec_copies = tile_copies(dec_tiles, dec_held, local_sems.at[1])
+    for copy in (*small, field_copy, *enc_copies):
+        copy.start()
     for peer in peers:
         pl.semaphore_signal(barrier, inc=1, device_id=peer, device_id_type=MESH)
 
-    enc_copies = tile_copies(enc_tiles, enc_held, local_sems.at[0])
-    dec_copies = tile_copies(dec_tiles, dec_held, local_sems.at[1])
-    for copy in enc_copies:
-        copy.start()
-
-    before, last = chain(enc_hid[...] & (HID_BLK - 1), enc_count[0])
-    before_back, last_back = chain(dec_src[...] & (SRC_BLK - 1), dec_count[0])
+    sums[NONE] = jnp.zeros((ROWS, TILE), jnp.float32)
+    for copy in small:
+        copy.wait()
+    before, last = chain(enc_hid[...] & (HID_BLK - 1), counts[:, 0:1])
+    before_back, last_back = chain(dec_src[...] & (SRC_BLK - 1), counts[:, 1:2])
     lane = lax.broadcasted_iota(jnp.int32, (CAP, TILE), 1)
     table[...] = jnp.where(
         lane == 0, before, jnp.where(lane == 1, last, jnp.where(lane == 2, before_back, last_back))
     )
-    sums[NONE] = jnp.zeros((ROWS, TILE), jnp.float32)
+    table_copy = pltpu.make_async_copy(table, table_s, local_sems.at[3, 0])
+    field_copy.wait()
     for s in range(SRC_BLK):
         value = field[s * ROWS : (s + 1) * ROWS]
         blocks[s] = value
         left[s] = split_pair(value)
-    table_copy = pltpu.make_async_copy(table, table_s, local_sems.at[2, 0])
-    table_copy.start()
+        if s == 1:
+            table_copy.start()
     for copy in dec_copies:
         copy.start()
     table_copy.wait()
-    for copy in enc_copies:
+    for chunk, copy in enumerate(enc_copies):
         copy.wait()
 
-    @pl.loop(0, CAP // UNROLL)
-    def _(step):
-        for i in range(UNROLL):
-            k = step * UNROLL + i
-            product = full_product(left[enc_src[k] & (SRC_BLK - 1)], stacked_tile(enc_held[k]))
-            sums[k] = sums[table_s[k, 0]] + product
+        @pl.loop(0, CAP // TILE_DMAS // UNROLL)
+        def _(step, chunk=chunk):
+            for i in range(UNROLL):
+                k = chunk * (CAP // TILE_DMAS) + step * UNROLL + i
+                product = full_product(left[enc_src[k] & (SRC_BLK - 1)], stacked_tile(enc_held[k]))
+                sums[k] = sums[table_s[k, 0]] + product
 
     @pl.loop(0, HID_BLK)
     def _(slot):
@@ -298,16 +324,34 @@
         )
 
     first = [[first_ring(c, i) for i in range(4)] for c in both]
+    def part_rows(ref, h, rows):
+        return ref.at[pl.ds(h * HALF, rows - HALF if h else HALF)]
+
     second = [
         RingSum(
             s,
             COLOURS[c][1],
-            lambda m, h, c=c: first_sum[c].at[m * 2 + h],
-            lambda n, c=c: second_in[c].at[n],
-            lambda h, c=c: second_sum[c].at[h],
+            lambda m, h, c=c: part_rows(pair_sum[c].at[m], h, CUTS[c][1]),
+            lambda n, c=c: second_in[c].at[
+                n, pl.ds(0, CUTS[c][1] - HALF if n in (1, 2, 5) else HALF)
+            ],
+            lambda h, c=c: part_rows(second_sum[c], h, CUTS[c][1]),
         )
         for c in both
     ]
+    pairs = {}
+
+    def pair_out(c, i):
+        there = shifted(COLOURS[c][1], order[i])
+        pairs[c, i] = s.start(
+            first_sum[c].at[there * 2 + other], pair_in[c].at[there], {Z: other}
+        )
+
+    def pair_back(c, i):
+        there = shifted(COLOURS[c][1], order[i])
+        pairs[c, i].wait_recv()
+        pair_sum[c][there] = first_sum[c][there * 2 + z] + pair_in[c][there]
+
     for i in (0, 1):
         for c in both:
             first[c][i].begin()
@@ -337,12 +381,20 @@
         if i >= 1:
             for c in both:
                 first[c][i - 1].end()
-                feed(c, i - 1)
-    swaps = []
+                pair_out(c, i - 1)
+        if i >= 2:
+            for c in both:
+                pair_back(c, i - 2)
+                feed(c, i - 2)
     for c in both:
         first[c][3].end()
+        pair_out(c, 3)
+    for c in both:
+        pair_back(c, 2)
+        feed(c, 2)
+    for c in both:
+        pair_back(c, 3)
         second[c].end()
-        swaps.append(s.start(second_sum[c].at[other], last_in[c], {Z: other}))
 
     row = lax.broadcasted_iota(jnp.int32, (ROWS, CH), 0)
     column = lax.broadcasted_iota(jnp.int32, (ROWS, CH), 1)
@@ -353,8 +405,7 @@
     )
     values, evens, odds = [], [], []
     for c in both:
-        swaps[c].wait_recv()
-        value = second_sum[c][z] + last_in[c][...]
+        value = second_sum[c][...]
         values.append(value)
         parity = lax.broadcasted_iota(jnp.int32, value.shape, 0) & 1
         square = value * value
@@ -370,60 +421,87 @@
             values[c] * scale[start : start + rows] * jnp.where(parity == 0, even, odd)
         )
 
-    def first_gather(c, step):
+    def outer_block(c, m, step, far):
+        there = shifted(COLOURS[c][1], step)
+        return hidden[c].at[m * 8 + there * 2 + (other if far else z)]
+
+    def inner_block(c, step):
         p, q = COLOURS[c]
-        there = shifted(q, step)
-        return RingGather(s, p, lambda m, h: hidden[c].at[m * 8 + there * 2 + h])
-
-    def second_gather(c):
-        p, q = COLOURS[c]
-        return RingGather(s, q, lambda m, h: hidden[c].at[where[p] * 8 + m * 2 + h])
-
-    outer = [[first_gather(c, step) for step in (0, 3, 1, 2)] for c in both]
-    inner = [second_gather(c) for c in both]
-    pairs = []
-    for c in both:
-        mine = inner[c].part(inner[c].me, z)
-        pairs.append(s.start(mine, mine, {Z: other}))
-        inner[c].give(z)
-    for c in both:
-        outer[c][0].give(z)
-    for c in both:
-        pairs[c].wait_recv()
-        inner[c].give(other)
-    for c in both:
-        outer[c][0].give(other)
-
-    def arrive(ring):
-        for copy in ring.rights + ring.lefts:
+        return hidden[c].at[where[p] * 8 + shifted(q, step) * 2 + z]
+
+    def send(block, axis, step):
+        return s.start(block, block, {axis: shifted(axis, step)})
+
+    inner, paired, outer, passed = {}, {}, {}, {}
+
+    def to_pair(c, step):
+        paired[c, step] = send(inner_block(c, step), Z, 1)
+
+    def to_line(c, step, far):
+        p = COLOURS[c][0]
+        block = outer_block(c, where[p], step, far)
+        outer[c, step, far] = [send(block, p, 1), send(block, p, -1)]
+
+    def along_line(c, step, far):
+        p = COLOURS[c][0]
+        from_left, from_right = outer[c, step, far]
+        if far:
+            from_right.wait_recv()
+            passed[c, step, far] = send(outer_block(c, shifted(p, 1), step, far), p, -1)
+        else:
+            from_left.wait_recv()
+            passed[c, step, far] = send(outer_block(c, shifted(p, -1), step, far), p, 1)
+
+    def settle_line(c, step, far):
+        outer[c, step, far][0 if far else 1].wait_recv()
+        passed[c, step, far].wait_recv()
+
+    for c in both:
+        q, mine = COLOURS[c][1], inner_block(c, 0)
+        inner[c] = [send(mine, q, 1), send(mine, q, -1)]
+        to_pair(c, 0)
+    for c in both:
+        to_line(c, 0, False)
+    for c in both:
+        q, rows = COLOURS[c][1], CUTS[c][1]
+        from_left, from_right = inner[c]
+        from_left.wait_recv()
+        inner[c] = [send(part_rows(inner_block(c, -1), 0, rows), q, 1)]
+        to_pair(c, -1)
+        from_right.wait_recv()
+        inner[c].append(send(part_rows(inner_block(c, 1), 1, rows), q, -1))
+        to_pair(c, 1)
+        to_line(c, -1, False)
+        to_line(c, 1, False)
+    for c in both:
+        paired[c, 0].wait_recv()
+        to_line(c, 0, True)
+    for c in both:
+        along_line(c, 0, False)
+    for c in both:
+        for copy in inner[c]:
             copy.wait_recv()
-
-    def forward(ring):
-        far_right, far_left = ring.part(ring.left[ring.axis], 0), ring.part(ring.right[ring.axis], 1)
-        ring.last = [s.start(far_right, far_right, ring.right), s.start(far_left, far_left, ring.left)]
-
-    for c in both:
-        arrive(inner[c])
-        forward(inner[c])
-        for ring in outer[c][1:3]:
-            ring.give(0)
-            ring.give(1)
-    for c in both:
-        arrive(outer[c][0])
-        forward(outer[c][0])
-    for c in both:
-        for copy in inner[c].last:
-            copy.wait_recv()
-        outer[c][3].give(0)
-        outer[c][3].give(1)
-    for n in (1, 2, 3):
-        for c in both:
-            arrive(outer[c][n])
-            forward(outer[c][n])
-    for n in range(4):
-        for c in both:
-            for copy in outer[c][n].last:
-                copy.wait_recv()
+        to_pair(c, 2)
+        to_line(c, 2, False)
+    for c in both:
+        for step in (-1, 1):
+            paired[c, step].wait_recv()
+            to_line(c, step, True)
+    for c in both:
+        along_line(c, -1, False)
+        along_line(c, 1, False)
+        along_line(c, 0, True)
+    for c in both:
+        paired[c, 2].wait_recv()
+        to_line(c, 2, True)
+    for c in both:
+        along_line(c, 2, False)
+        along_line(c, -1, True)
+        along_line(c, 1, True)
+    for c in both:
+        along_line(c, 2, True)
+    for key in passed:
+        settle_line(*key)
 
     @pl.loop(0, CAP // UNROLL)
     def _(step):
@@ -447,11 +525,6 @@
             crossing[step, c] = s.start(
                 back[c].at[twin * 4 + m], core_in[c].at[m], {CORE: twin}
             )
-    for step in order:
-        m = lax.rem(zh + step, 4)
-        for c in both:
-            crossing[step, c].wait_recv()
-            core_sum[c][m] = back[c][core * 4 + m] + core_in[c][m]
     column_ring = RingSum(
         s,
         ZH,
@@ -459,9 +532,27 @@
         lambda n: ring_in[(0, 1, 1, 0, 0, 1)[n]].at[(0, 0, 1, 1, 2, 2)[n]],
         lambda h: result[h].at[core * 4 + zh],
     )
-    column_ring.begin()
+    for step in order:
+        m = lax.rem(zh + step, 4)
+        for c in both:
+            crossing[step, c].wait_recv()
+            core_sum[c][m] = back[c][core * 4 + m] + core_in[c][m]
+        if step == 2:
+            column_ring.begin_far()
+        elif step == 1:
+            column_ring.begin_right()
+        elif step == 3:
+            column_ring.begin_left()
     column_ring.middle()
     column_ring.end()
+
+    def arrive(ring):
+        for copy in ring.rights + ring.lefts:
+            copy.wait_recv()
+
+    def forward(ring):
+        far_right, far_left = ring.part(ring.left[ring.axis], 0), ring.part(ring.right[ring.axis], 1)
+        ring.last = [s.start(far_right, far_right, ring.right), s.start(far_left, far_left, ring.left)]
 
     gather = RingGather(s, ZH, lambda m, h: result[h].at[core * 4 + m])
     gather.give(0)
@@ -513,16 +604,18 @@
     rms[...] = jnp.sqrt(squares[3] * (1.0 / TOTAL_POINTS) + EPSILON)
     for copy in twins:
         copy.wait_recv()
+    s.finish()
+
+
+def assemble_kernel(result_0, result_1, rms, out, rms_out):
     for i in range(SRC_BLK):
-        for c in both:
-            start, rows = CUTS[c]
-            out[i * ROWS + start : i * ROWS + start + rows] = result[c][i]
-    s.finish()
+        for (start, rows), part in zip(CUTS, (result_0, result_1)):
+            out[i * ROWS + start : i * ROWS + start + rows] = part[i]
+    rms_out[...] = rms[0:1, 0:CH]
 
 
 VMEM = pl.BlockSpec(memory_space=pltpu.VMEM)
-SMEM = pl.BlockSpec(memory_space=pltpu.SMEM)
-ANY = pl.BlockSpec(memory_space=pl.ANY)
+HBM = pl.BlockSpec(memory_space=pltpu.HBM)
 
 
 def coloured(*lead):
@@ -543,15 +636,19 @@
 ):
     rows = source_field.transpose(0, 2, 1, 3).reshape(SRC_BLK * ROWS, TILE)
     held = pltpu.VMEM((CAP, TILE, TILE), jnp.float32)
-    returned, rms = pl.pallas_call(
+    pieces = pl.pallas_call(
         whole_kernel,
-        out_shape=(
-            jax.ShapeDtypeStruct((SRC_BLK * ROWS, TILE), jnp.float32),
-            jax.ShapeDtypeStruct((8, TILE), jnp.float32),
-        ),
-        in_specs=[SMEM, VMEM, SMEM, VMEM, SMEM, SMEM, VMEM, VMEM, ANY, ANY],
-        out_specs=(VMEM, VMEM),
+        out_shape=(*coloured(SRC_BLK), pltpu.VMEM((8, TILE), jnp.float32)),
+        in_specs=[HBM] * 9,
+        out_specs=(VMEM, VMEM, VMEM),
         scratch_shapes=[
+            pltpu.SMEM((CAP,), jnp.int32),
+            pltpu.VMEM((1, CAP), jnp.int32),
+            pltpu.VMEM((1, 2), jnp.int32),
+            pltpu.VMEM((1, CAP), jnp.int32),
+            pltpu.SMEM((CAP,), jnp.int32),
+            pltpu.VMEM((SRC_BLK * ROWS, TILE), jnp.float32),
+            pltpu.VMEM((1, CH), jnp.float32),
             held,
             held,
             pltpu.VMEM((CAP, TILE), jnp.int32),
@@ -563,18 +660,18 @@
             *coloured(HID_BLK),
             *coloured(4, 6),
             *coloured(8),
-            *coloured(6),
-            *coloured(2),
+            *coloured(4),
+            *coloured(4),
+            *[pltpu.VMEM((6, 56, TILE), jnp.float32)] * 2,
             *coloured(),
             *coloured(HID_BLK),
             *coloured(SRC_BLK),
             *coloured(4),
             *coloured(4),
             *coloured(3),
-            *coloured(SRC_BLK),
             pltpu.VMEM((4, 8, TILE), jnp.float32),
             pltpu.VMEM((21, 8, TILE), jnp.float32),
-            pltpu.SemaphoreType.DMA((3, TILE_DMAS)),
+            pltpu.SemaphoreType.DMA((4, 8)),
             pltpu.SemaphoreType.DMA((N_SEMS,)),
             pltpu.SemaphoreType.DMA((N_SEMS,)),
         ],
@@ -582,17 +679,25 @@
     )(
         enc_src_block,
         enc_hid_block.reshape(1, CAP),
-        enc_count,
+        jnp.concatenate([enc_count, dec_count]).reshape(1, 2),
         dec_src_block.reshape(1, CAP),
         dec_hid_block,
-        dec_count,
         rows,
         hidden_gain.reshape(1, CH),
         enc_tiles,
         dec_tiles,
     )
+    returned, rms = pl.pallas_call(
+        assemble_kernel,
+        out_shape=(
+            jax.ShapeDtypeStruct((SRC_BLK * ROWS, TILE), jnp.float32),
+            jax.ShapeDtypeStruct((1, CH), jnp.float32),
+        ),
+        in_specs=[VMEM] * 3,
+        out_specs=(VMEM, VMEM),
+    )(*[pltpu.with_memory_space_constraint(piece, pltpu.VMEM) for piece in pieces])
     returned = returned.reshape(SRC_BLK, CH, BATCH, TILE).transpose(0, 2, 1, 3)
-    return returned, rms[0, :CH]
+    return returned, rms.reshape(CH)
 
 
 def solution(mesh):

time: 98.3 us -> 90.4 us (0.920)
  Pallas kernels: 92.5 us -> 88 us
  local copies, waits for them, and re-layouts: 3.26 us -> 0 us
    pallas_call x1 -> x2, Pallas kernels: 92.5 us -> 88 us  [the longest x1 87.1 us: body(): pl.pallas_call(whole_kernel, out_shape=(*coloured(SRC_BLK), pltpu.VMEM((8...]
    unnamed x1 -> x0, local copies, waits for them, and re-layouts: 2.08 us -> none
    squeeze x1 -> x0, local copies, waits for them, and re-layouts: 1.18 us -> none  [body(): return (returned, rms[0, :CH])]
where the time goes in v3:
time: 90.4 us; the launch traced here: 90.5 us
  Pallas kernels  88 us (97%)
  between operations  1.93 us (2%)
    pallas_call x1, Pallas kernels, body(): pl.pallas_call(whole_kernel, out_shape=(*coloured(SRC_BLK), pltpu.VMEM((8...  87.1 us

profile of v3, /device:TPU:1, one launch (start us, length us, event | category | flops | bytes accessed | tf_op | source)
XLA Modules:
  0.0 90.5 jit_solution(17173752353053111399)
XLA Ops:
  1.9 0.6 add_bitcast_fusion.counts_any
  2.5 87.1 %shard_map.113 = (f32[8,96,128]{2,1,0:T(8,128)S(1)}, f32[8,100,128]{2,1,0:T(8,128)S(1)}, f32[8,128]{1,0:T(8,128)S(1)}) custom-call(s32[32]{0:T(128)} %enc_src_any.1, s32[1,32]{1,0:T(1,128)} %bitcast.13, s32[1,2]{1,0:T(1,128)} %add_bitcast_fusion.counts_any, s32[1,32]{1,0:T(1,128)} %bitcast.14, s32[32]{0:T(128)} %dec_hid_any.1, f32[1568,128]{1,0:T(8,128)} %bitcast.12, ...), custom_call_target="tpu_custom_call" | custom-call | tf_op jit(solution)/shard_map/pallas_call | solution.py:639
  89.6 0.9 %shard_map.114 = (f32[1568,128]{1,0:T(8,128)}, f32[1,98]{1,0:T(1,128)}) custom-call(f32[8,96,128]{2,1,0:T(8,128)S(1)} %get-tuple-element.7.result_0, f32[8,100,128]{2,1,0:T(8,128)S(1)} %get-tuple-element.8.result_1, f32[8,128]{1,0:T(8,128)S(1)} %get-tuple-element.9.rms), custom_call_target="tpu_custom_call" | custom-call | tf_op jit(solution)/shard_map/pallas_call | solution.py:690

commit v4 on v3

--- a/solution.py
+++ b/solution.py
@@ -80,7 +80,7 @@
     lane = lax.broadcasted_iota(jnp.int32, (CAP, CAP), 1)
     along = jnp.broadcast_to(targets, (CAP, CAP))
     down = jnp.sum(jnp.where(row == lane, along, 0), axis=1, keepdims=True)
-    live = lane < jnp.broadcast_to(count, (CAP, CAP))
+    live = lane < count
     before = jnp.max(jnp.where(live & (lane < row) & (along == down), lane, -1), axis=1, keepdims=True)
     last = jnp.max(jnp.where(live & (along == row), lane, -1), axis=1, keepdims=True)
     return jnp.where(before < 0, NONE, before), jnp.where(last < 0, NONE, last)
@@ -156,25 +156,13 @@
         self.total(1)[...] = (part(me, 1)[...] + landed(2)[...]) + landed(5)[...]
 
 
-class RingGather:
-    def __init__(self, sender, axis, part):
-        self.s, self.axis, self.part = sender, axis, part
-        self.me = lax.axis_index(axis)
-        self.right, self.left = {axis: shifted(axis, 1)}, {axis: shifted(axis, -1)}
-        self.rights, self.lefts = [], []
-
-    def give(self, half):
-        mine = self.part(self.me, half)
-        self.rights.append(self.s.start(mine, mine, self.right))
-        self.lefts.append(self.s.start(mine, mine, self.left))
-
-
 def whole_kernel(
     enc_src_any,
     enc_hid_any,
-    counts_any,
+    enc_count,
     dec_src_any,
     dec_hid_any,
+    dec_count,
     field_any,
     gain_any,
     enc_tiles,
@@ -184,7 +172,6 @@
     rms,
     enc_src,
     enc_hid,
-    counts,
     dec_src,
     dec_hid,
     field,
@@ -256,7 +243,6 @@
             (
                 (enc_src_any, enc_src),
                 (enc_hid_any, enc_hid),
-                (counts_any, counts),
                 (dec_src_any, dec_src),
                 (dec_hid_any, dec_hid),
                 (gain_any, gain),
@@ -274,8 +260,8 @@
     sums[NONE] = jnp.zeros((ROWS, TILE), jnp.float32)
     for copy in small:
         copy.wait()
-    before, last = chain(enc_hid[...] & (HID_BLK - 1), counts[:, 0:1])
-    before_back, last_back = chain(dec_src[...] & (SRC_BLK - 1), counts[:, 1:2])
+    before, last = chain(enc_hid[...] & (HID_BLK - 1), enc_count[0])
+    before_back, last_back = chain(dec_src[...] & (SRC_BLK - 1), dec_count[0])
     lane = lax.broadcasted_iota(jnp.int32, (CAP, TILE), 1)
     table[...] = jnp.where(
         lane == 0, before, jnp.where(lane == 1, last, jnp.where(lane == 2, before_back, last_back))
@@ -546,17 +532,13 @@
     column_ring.middle()
     column_ring.end()
 
-    def arrive(ring):
-        for copy in ring.rights + ring.lefts:
-            copy.wait_recv()
-
-    def forward(ring):
-        far_right, far_left = ring.part(ring.left[ring.axis], 0), ring.part(ring.right[ring.axis], 1)
-        ring.last = [s.start(far_right, far_right, ring.right), s.start(far_left, far_left, ring.left)]
-
-    gather = RingGather(s, ZH, lambda m, h: result[h].at[core * 4 + m])
-    gather.give(0)
-    gather.give(1)
+    def own_half(step, h):
+        return result[h].at[core * 4 + lax.rem(zh + step, 4)]
+
+    to_right = [send(own_half(0, 0), ZH, 1)]
+    to_left = [send(own_half(0, 1), ZH, -1)]
+    to_right.append(send(own_half(0, 1), ZH, 1))
+    to_left.append(send(own_half(0, 0), ZH, -1))
     total = None
     for c in both:
         start, rows = CUTS[c]
@@ -568,11 +550,11 @@
         total = part if total is None else total + part
     squares[0] = jnp.broadcast_to(total, (8, TILE))
 
-    def to_twin(m, c):
-        block = result[c].at[core * 4 + m]
+    def to_twin(step, c):
+        block = own_half(step, c)
         return s.start(block, block, {CORE: twin})
 
-    twins = [to_twin(zh, c) for c in both]
+    twins = [to_twin(0, c) for c in both]
 
     def exchange(stage, first_slot, those):
         return [
@@ -588,18 +570,21 @@
         squares[stage + 1] = value
 
     copies = exchange(0, 0, lines[0])
-    arrive(gather)
-    forward(gather)
     collect(0, 0, copies)
     copies = exchange(1, 3, lines[1])
-    for step in (1, 3):
-        for c in both:
-            twins.append(to_twin(lax.rem(zh + step, 4), c))
+    to_right[0].wait_recv()
+    passing = [send(own_half(3, 0), ZH, 1)]
+    to_left[0].wait_recv()
+    passing.append(send(own_half(1, 1), ZH, -1))
+    twins += [to_twin(3, 0), to_twin(1, 1)]
     collect(1, 3, copies)
     copies = exchange(2, 6, stack)
-    for c, copy in zip(both, gather.last):
-        copy.wait_recv()
-        twins.append(to_twin(lax.rem(zh + 2, 4), c))
+    to_right[1].wait_recv()
+    to_left[1].wait_recv()
+    twins += [to_twin(3, 1), to_twin(1, 0)]
+    for c in both:
+        passing[c].wait_recv()
+        twins.append(to_twin(2, c))
     collect(2, 6, copies)
     rms[...] = jnp.sqrt(squares[3] * (1.0 / TOTAL_POINTS) + EPSILON)
     for copy in twins:
@@ -616,6 +601,7 @@
 
 VMEM = pl.BlockSpec(memory_space=pltpu.VMEM)
 HBM = pl.BlockSpec(memory_space=pltpu.HBM)
+SMEM = pl.BlockSpec(memory_space=pltpu.SMEM)
 
 
 def coloured(*lead):
@@ -639,12 +625,11 @@
     pieces = pl.pallas_call(
         whole_kernel,
         out_shape=(*coloured(SRC_BLK), pltpu.VMEM((8, TILE), jnp.float32)),
-        in_specs=[HBM] * 9,
+        in_specs=[HBM, HBM, SMEM, HBM, HBM, SMEM, HBM, HBM, HBM, HBM],
         out_specs=(VMEM, VMEM, VMEM),
         scratch_shapes=[
             pltpu.SMEM((CAP,), jnp.int32),
             pltpu.VMEM((1, CAP), jnp.int32),
-            pltpu.VMEM((1, 2), jnp.int32),
             pltpu.VMEM((1, CAP), jnp.int32),
             pltpu.SMEM((CAP,), jnp.int32),
             pltpu.VMEM((SRC_BLK * ROWS, TILE), jnp.float32),
@@ -679,9 +664,10 @@
     )(
         enc_src_block,
         enc_hid_block.reshape(1, CAP),
-        jnp.concatenate([enc_count, dec_count]).reshape(1, 2),
+        enc_count,
         dec_src_block.reshape(1, CAP),
         dec_hid_block,
+        dec_count,
         rows,
         hidden_gain.reshape(1, CH),
         enc_tiles,

time: 90.4 us -> 85.6 us (0.947)
  Pallas kernels: 88 us -> 83 us
    pallas_call x1, Pallas kernels: 87.1 us -> 82.1 us  [body(): pl.pallas_call(whole_kernel, out_shape=(*coloured(SRC_BLK), pltpu.VMEM((8...]
where the time goes in v4:
time: 85.6 us; the launch traced here: 84.9 us
  Pallas kernels  83 us (97%)
  between operations  1.93 us (2%)
    pallas_call x1, Pallas kernels, body(): pl.pallas_call(whole_kernel, out_shape=(*coloured(SRC_BLK), pltpu.VMEM((8...  82.1 us

profile of v4, /device:TPU:1, one launch (start us, length us, event | category | flops | bytes accessed | tf_op | source)
XLA Modules:
  0.0 84.9 jit_solution(16870510215325808737)
XLA Ops:
  1.9 82.1 %shard_map.113 = (f32[8,96,128]{2,1,0:T(8,128)S(1)}, f32[8,100,128]{2,1,0:T(8,128)S(1)}, f32[8,128]{1,0:T(8,128)S(1)}) custom-call(s32[32]{0:T(128)} %enc_src_any.1, s32[1,32]{1,0:T(1,128)} %bitcast.11, s32[1]{0:T(128)S(6)} %copy.12.enc_count, s32[1,32]{1,0:T(1,128)} %bitcast.12, s32[32]{0:T(128)} %dec_hid_any.1, s32[1]{0:T(128)S(6)} %copy.13.dec_count, ...), custom_call_target="tpu_custom_call" | custom-call | tf_op jit(solution)/shard_map/pallas_call | solution.py:625
  84.0 0.9 %shard_map.114 = (f32[1568,128]{1,0:T(8,128)}, f32[1,98]{1,0:T(1,128)}) custom-call(f32[8,96,128]{2,1,0:T(8,128)S(1)} %get-tuple-element.7.result_0, f32[8,100,128]{2,1,0:T(8,128)S(1)} %get-tuple-element.8.result_1, f32[8,128]{1,0:T(8,128)S(1)} %get-tuple-element.9.rms), custom_call_target="tpu_custom_call" | custom-call | tf_op jit(solution)/shard_map/pallas_call | solution.py:676

commit v5 on v4

v5 whole, which is shorter than its diff:
```python
import jax
import jax.numpy as jnp
from jax import lax
from jax.experimental import pallas as pl
from jax.experimental.pallas import tpu as pltpu
from jax.sharding import Mesh
from jax.sharding import PartitionSpec as P

CH = 98
BATCH = 2
TILE = 128
ROWS = CH * BATCH
SRC_BLK = 8
HID_BLK = 32
CAP = 32
NONE = CAP
TOTAL_POINTS = 256 * BATCH * TILE
EPSILON = 1e-06
AXES = ("src_0", "src_1", "src_2", "hid_0", "hid_1")
SRC = ("src_0", "src_1", "src_2")
SIZES = {"src_0": 4, "src_1": 2, "src_2": 4, "hid_0": 4, "hid_1": 2}
MESH = pl.DeviceIdType.MESH
TILE_DMAS = 4
UNROLL = 4
N_SEMS = 341

X, Z, Y, ZH, CORE = AXES
STEP = 112
CUTS = ((0, 48), (48, 50))
HALF = 24
COLOURS = ((X, Y), (Y, X))
BOTH = (0, 1)
ORDER = (2, 1, 3, 0)


def slot_of(block, colour):
    x, z, y = block >> 3, (block >> 2) & 1, block & 3
    if colour == 0:
        return x * 8 + y * 2 + z
    return y * 8 + x * 2 + z


def block_in(slot, colour):
    p, q, z = slot >> 3, (slot >> 1) & 3, slot & 1
    if colour == 0:
        return p * 8 + z * 4 + q
    return q * 8 + z * 4 + p


def split_pair(value):
    high = value.astype(jnp.bfloat16)
    low = (value - high.astype(jnp.float32)).astype(jnp.bfloat16)
    return jnp.concatenate([high, low], axis=1)


def stacked_tile(tile):
    row = split_pair(tile)
    return jnp.concatenate([row, row], axis=0)


def full_product(left, right):
    both = jnp.dot(left, right, preferred_element_type=jnp.float32)
    return both[:, :TILE] + both[:, TILE:]


def tile_copies(tiles, held, sems):
    part = CAP // TILE_DMAS
    return [
        pltpu.make_async_copy(
            tiles.at[pl.ds(i * part, part)], held.at[pl.ds(i * part, part)], sems.at[i]
        )
        for i in range(TILE_DMAS)
    ]


def shifted(axis, step):
    size = SIZES[axis]
    return lax.rem(lax.axis_index(axis) + (step + size), size)


def chain(targets, count):
    row = lax.broadcasted_iota(jnp.int32, (CAP, CAP), 0)
    lane = lax.broadcasted_iota(jnp.int32, (CAP, CAP), 1)
    along = jnp.broadcast_to(targets, (CAP, CAP))
    down = jnp.sum(jnp.where(row == lane, along, 0), axis=1, keepdims=True)
    live = lane < count
    before = jnp.max(jnp.where(live & (lane < row) & (along == down), lane, -1), axis=1, keepdims=True)
    last = jnp.max(jnp.where(live & (along == row), lane, -1), axis=1, keepdims=True)
    return jnp.where(before < 0, NONE, before), jnp.where(last < 0, NONE, last)


class Sender:
    def __init__(self, send_sems, recv_sems):
        self.send_sems, self.recv_sems, self.count, self.sent = send_sems, recv_sems, 0, []

    def start(self, src, dst, where):
        i = self.count
        self.count += 1
        copy = pltpu.make_async_remote_copy(
            src_ref=src,
            dst_ref=dst,
            send_sem=self.send_sems.at[i],
            recv_sem=self.recv_sems.at[i],
            device_id=where,
            device_id_type=MESH,
        )
        copy.start()
        self.sent.append(copy)
        return copy

    def along(self, block, axis, step):
        return self.start(block, block, {axis: shifted(axis, step)})

    def finish(self):
        for copy in self.sent:
            copy.wait_send()


class RingSum:
    def __init__(self, sender, axis, part, landed, total):
        self.s, self.axis, self.part, self.landed, self.total = sender, axis, part, landed, total
        self.right, self.left = {axis: shifted(axis, 1)}, {axis: shifted(axis, -1)}

    def begin_far(self):
        opposite = shifted(self.axis, 2)
        self.r1 = self.s.start(self.part(opposite, 0), self.landed(0), self.right)
        self.l1 = self.s.start(self.part(opposite, 1), self.landed(1), self.left)

    def begin_right(self):
        self.r2 = self.s.start(self.part(self.right[self.axis], 1), self.landed(2), self.right)

    def begin_left(self):
        self.l2 = self.s.start(self.part(self.left[self.axis], 0), self.landed(3), self.left)

    def begin(self):
        self.begin_far()
        self.begin_right()
        self.begin_left()

    def middle_right(self):
        self.r1.wait_recv()
        self.landed(0)[...] = self.landed(0)[...] + self.part(self.right[self.axis], 0)[...]
        self.r3 = self.s.start(self.landed(0), self.landed(4), self.right)

    def middle_left(self):
        self.l1.wait_recv()
        self.landed(1)[...] = self.landed(1)[...] + self.part(self.left[self.axis], 1)[...]
        self.l3 = self.s.start(self.landed(1), self.landed(5), self.left)

    def middle(self):
        self.middle_right()
        self.middle_left()

    def end(self):
        me = lax.axis_index(self.axis)
        landed, part = self.landed, self.part
        self.r2.wait_recv()
        self.l2.wait_recv()
        self.r3.wait_recv()
        self.total(0)[...] = (part(me, 0)[...] + landed(3)[...]) + landed(4)[...]
        self.l3.wait_recv()
        self.total(1)[...] = (part(me, 1)[...] + landed(2)[...]) + landed(5)[...]


def part_rows(ref, h, rows):
    return ref.at[pl.ds(h * HALF, rows - HALF if h else HALF)]


def whole_kernel(
    enc_src_any,
    enc_hid_any,
    enc_count,
    dec_src_any,
    dec_hid_any,
    dec_count,
    field_any,
    gain_any,
    enc_tiles,
    dec_tiles,
    result_00,
    result_01,
    result_10,
    result_11,
    rms,
    enc_src,
    enc_hid,
    dec_src,
    dec_hid,
    field,
    gain,
    enc_held,
    dec_held,
    table,
    table_s,
    blocks,
    left,
    right,
    sums,
    partial,
    first_in,
    first_sum,
    pair_in,
    pair_sum,
    second_in,
    second_sum,
    hidden,
    back,
    core_in,
    core_sum,
    ring_in,
    squares,
    square_in,
    local_sems,
    send_sems,
    recv_sems,
):
    result = ((result_00, result_01), (result_10, result_11))
    x, y, z = lax.axis_index(X), lax.axis_index(Y), lax.axis_index(Z)
    zh, core = lax.axis_index(ZH), lax.axis_index(CORE)
    other, twin = 1 - z, 1 - core
    where = {X: x, Y: y}

    lines = [[{axis: shifted(axis, i)} for i in (1, 2, 3)] for axis in (X, Y)]
    stack = [
        {Z: lax.rem(z + dz, 2), ZH: lax.rem(zh + dh, 4), CORE: lax.rem(core + dc, 2)}
        for dz in range(2)
        for dh in range(4)
        for dc in range(2)
        if dz + dh + dc
    ]
    peers = lines[0] + lines[1] + stack
    barrier = pltpu.get_barrier_semaphore()
    small = [
        pltpu.make_async_copy(there, here, local_sems.at[2, i])
        for i, (there, here) in enumerate(
            (
                (enc_src_any, enc_src),
                (enc_hid_any, enc_hid),
                (dec_src_any, dec_src),
                (dec_hid_any, dec_hid),
                (gain_any, gain),
            )
        )
    ]
    field_copy = pltpu.make_async_copy(field_any, field, local_sems.at[2, 7])
    enc_copies = tile_copies(enc_tiles, enc_held, local_sems.at[0])
    dec_copies = tile_copies(dec_tiles, dec_held, local_sems.at[1])
    for copy in (*small, field_copy, *enc_copies):
        copy.start()
    for peer in peers:
        pl.semaphore_signal(barrier, inc=1, device_id=peer, device_id_type=MESH)

    sums[NONE] = jnp.zeros((STEP + CH, TILE), jnp.float32)
    for copy in small:
        copy.wait()
    before, last = chain(enc_hid[...] & (HID_BLK - 1), enc_count[0])
    before_back, last_back = chain(dec_src[...] & (SRC_BLK - 1), dec_count[0])
    lane = lax.broadcasted_iota(jnp.int32, (CAP, TILE), 1)
    table[...] = jnp.where(
        lane == 0, before, jnp.where(lane == 1, last, jnp.where(lane == 2, before_back, last_back))
    )
    table_copy = pltpu.make_async_copy(table, table_s, local_sems.at[3, 0])
    field_copy.wait()
    for i in range(SRC_BLK):
        left[i, CH:STEP] = jnp.zeros((STEP - CH, 2 * TILE), jnp.bfloat16)
        for b in BOTH:
            value = field[pl.ds(i * ROWS + b, CH, stride=2)]
            blocks[b, i] = value
            left[i, b * STEP : b * STEP + CH] = split_pair(value)
        if i == 1:
            table_copy.start()
    for copy in dec_copies:
        copy.start()
    table_copy.wait()
    for chunk, copy in enumerate(enc_copies):
        copy.wait()

        @pl.loop(0, CAP // TILE_DMAS // UNROLL)
        def _(step, chunk=chunk):
            for i in range(UNROLL):
                k = chunk * (CAP // TILE_DMAS) + step * UNROLL + i
                product = full_product(left[enc_src[k] & (SRC_BLK - 1)], stacked_tile(enc_held[k]))
                sums[k] = sums[table_s[k, 0]] + product

    @pl.loop(0, HID_BLK)
    def _(slot):
        for c in BOTH:
            start, rows = CUTS[c]
            k = table_s[block_in(slot, c), 1]
            for b in BOTH:
                partial[b][c][slot] = sums[k, b * STEP + start : b * STEP + start + rows]

    pl.semaphore_wait(barrier, len(peers))
    s = Sender(send_sems, recv_sems)
    identity = lax.broadcasted_iota(jnp.int32, (CH, CH), 0) == lax.broadcasted_iota(
        jnp.int32, (CH, CH), 1
    )
    scale = jnp.sum(
        jnp.where(identity, jnp.broadcast_to(gain[...], (CH, CH)), 0.0), axis=1, keepdims=True
    )

    def reduce_steps(b):
        def first_ring(c, i):
            p, q = COLOURS[c]
            there = shifted(q, ORDER[i])
            return RingSum(
                s,
                p,
                lambda m, h: partial[b][c].at[m * 8 + there * 2 + h],
                lambda n: first_in[b][c].at[i, n],
                lambda h: first_sum[b][c].at[there * 2 + h],
            )

        def second_ring(c):
            rows = CUTS[c][1]
            return RingSum(
                s,
                COLOURS[c][1],
                lambda m, h: part_rows(pair_sum[b][c].at[m], h, rows),
                lambda n: second_in[b][c].at[n, pl.ds(0, rows - HALF if n in (1, 2, 5) else HALF)],
                lambda h: part_rows(second_sum[b][c], h, rows),
            )

        first = [[first_ring(c, i) for i in range(4)] for c in BOTH]
        second = [second_ring(c) for c in BOTH]
        pairs = {}

        def settle(i):
            for c in BOTH:
                first[c][i].end()
                there = shifted(COLOURS[c][1], ORDER[i])
                pairs[c, i] = s.start(
                    first_sum[b][c].at[there * 2 + other], pair_in[b][c].at[there], {Z: other}
                )

        def pair_back(c, i):
            there = shifted(COLOURS[c][1], ORDER[i])
            pairs[c, i].wait_recv()
            pair_sum[b][c][there] = first_sum[b][c][there * 2 + z] + pair_in[b][c][there]

        for i in (0, 1):
            for c in BOTH:
                first[c][i].begin()
        yield
        for c in BOTH:
            first[c][0].middle()
            first[c][2].begin()
        yield
        for c in BOTH:
            first[c][1].middle()
            first[c][3].begin()
        settle(0)
        yield
        for c in BOTH:
            first[c][2].middle()
        settle(1)
        for c in BOTH:
            pair_back(c, 0)
            second[c].begin_far()
        yield
        for c in BOTH:
            first[c][3].middle()
        settle(2)
        for c in BOTH:
            pair_back(c, 1)
            second[c].begin_right()
            second[c].middle_right()
        yield
        settle(3)
        for c in BOTH:
            pair_back(c, 2)
            second[c].begin_left()
            second[c].middle_left()
        yield
        squares_sum = None
        for c in BOTH:
            pair_back(c, 3)
            second[c].end()
            value = second_sum[b][c][...]
            square = jnp.sum(value * value, axis=0, keepdims=True)
            squares_sum = square if squares_sum is None else squares_sum + square
        factor = lax.rsqrt(squares_sum * (1.0 / CH) + EPSILON)
        for c in BOTH:
            start, rows = CUTS[c]
            p, q = (where[axis] for axis in COLOURS[c])
            hidden[b][c][p * 8 + q * 2 + z] = (
                second_sum[b][c][...] * scale[start : start + rows] * factor
            )

    def gather_steps(b):
        inner, paired, outer, passed = {}, {}, {}, {}

        def outer_block(c, m, step, far):
            there = shifted(COLOURS[c][1], step)
            return hidden[b][c].at[m * 8 + there * 2 + (other if far else z)]

        def inner_block(c, step):
            p, q = COLOURS[c]
            return hidden[b][c].at[where[p] * 8 + shifted(q, step) * 2 + z]

        def to_pair(c, step):
            paired[c, step] = s.along(inner_block(c, step), Z, 1)

        def to_line(c, step, far):
            p = COLOURS[c][0]
            block = outer_block(c, where[p], step, far)
            outer[c, step, far] = [s.along(block, p, 1), s.along(block, p, -1)]

        def along_line(c, step, far):
            p = COLOURS[c][0]
            from_left, from_right = outer[c, step, far]
            if far:
                from_right.wait_recv()
                passed[c, step, far] = s.along(outer_block(c, shifted(p, 1), step, far), p, -1)
            else:
                from_left.wait_recv()
                passed[c, step, far] = s.along(outer_block(c, shifted(p, -1), step, far), p, 1)

        for c in BOTH:
            q, mine = COLOURS[c][1], inner_block(c, 0)
            inner[c] = [s.along(mine, q, 1), s.along(mine, q, -1)]
            to_pair(c, 0)
        for c in BOTH:
            to_line(c, 0, False)
        yield
        for c in BOTH:
            q, rows = COLOURS[c][1], CUTS[c][1]
            from_left, from_right = inner[c]
            from_left.wait_recv()
            inner[c] = [s.along(part_rows(inner_block(c, -1), 0, rows), q, 1)]
            to_pair(c, -1)
            from_right.wait_recv()
            inner[c].append(s.along(part_rows(inner_block(c, 1), 1, rows), q, -1))
            to_pair(c, 1)
            to_line(c, -1, False)
            to_line(c, 1, False)
        yield
        for c in BOTH:
            paired[c, 0].wait_recv()
            to_line(c, 0, True)
        for c in BOTH:
            along_line(c, 0, False)
        yield
        for c in BOTH:
            for copy in inner[c]:
                copy.wait_recv()
            to_pair(c, 2)
            to_line(c, 2, False)
        yield
        for c in BOTH:
            for step in (-1, 1):
                paired[c, step].wait_recv()
                to_line(c, step, True)
        for c in BOTH:
            along_line(c, -1, False)
            along_line(c, 1, False)
            along_line(c, 0, True)
        yield
        for c in BOTH:
            paired[c, 2].wait_recv()
            to_line(c, 2, True)
        for c in BOTH:
            along_line(c, 2, False)
            along_line(c, -1, True)
            along_line(c, 1, True)
        yield
        for c in BOTH:
            along_line(c, 2, True)
        yield
        for c, step, far in passed:
            outer[c, step, far][0 if far else 1].wait_recv()
            passed[c, step, far].wait_recv()

    def decode(b):
        @pl.loop(0, CAP // UNROLL)
        def _(step):
            for i in range(UNROLL):
                k = step * UNROLL + i
                block = dec_hid[k] & (HID_BLK - 1)
                pieces = [split_pair(hidden[b][c][slot_of(block, c)]) for c in BOTH]
                product = full_product(jnp.concatenate(pieces, axis=0), right[k])
                here = slice(b * STEP, b * STEP + CH)
                sums[k, here] = sums[table_s[k, 2], here] + product

        @pl.loop(0, SRC_BLK)
        def _(i):
            k = table_s[i, 3]
            for c in BOTH:
                start, rows = CUTS[c]
                back[b][c][i] = sums[k, b * STEP + start : b * STEP + start + rows]

    def column_steps(b):
        crossing = {}
        for step in ORDER:
            m = lax.rem(zh + step, 4)
            for c in BOTH:
                crossing[step, c] = s.start(
                    back[b][c].at[twin * 4 + m], core_in[b][c].at[m], {CORE: twin}
                )
        yield
        ring = RingSum(
            s,
            ZH,
            lambda m, h: core_sum[b][h].at[m],
            lambda n: ring_in[b][(0, 1, 1, 0, 0, 1)[n]].at[(0, 0, 1, 1, 2, 2)[n]],
            lambda h: result[b][h].at[core * 4 + zh],
        )
        for step in ORDER:
            m = lax.rem(zh + step, 4)
            for c in BOTH:
                crossing[step, c].wait_recv()
                core_sum[b][c][m] = back[b][c][core * 4 + m] + core_in[b][c][m]
            if step == 2:
                ring.begin_far()
            elif step == 1:
                ring.begin_right()
            elif step == 3:
                ring.begin_left()
        yield
        ring.middle()
        yield
        ring.end()

        def own_half(step, h):
            return result[b][h].at[core * 4 + lax.rem(zh + step, 4)]

        def to_twin(step, c):
            return s.along(own_half(step, c), CORE, 1)

        to_right = [s.along(own_half(0, 0), ZH, 1)]
        to_left = [s.along(own_half(0, 1), ZH, -1)]
        to_right.append(s.along(own_half(0, 1), ZH, 1))
        to_left.append(s.along(own_half(0, 0), ZH, -1))
        twins = [to_twin(0, c) for c in BOTH]
        yield
        to_right[0].wait_recv()
        passing = [s.along(own_half(3, 0), ZH, 1)]
        to_left[0].wait_recv()
        passing.append(s.along(own_half(1, 1), ZH, -1))
        twins += [to_twin(3, 0), to_twin(1, 1)]
        yield
        to_right[1].wait_recv()
        to_left[1].wait_recv()
        twins += [to_twin(3, 1), to_twin(1, 0)]
        for c in BOTH:
            passing[c].wait_recv()
            twins.append(to_twin(2, c))
        yield
        for copy in twins:
            copy.wait_recv()

    def own_squares(b):
        line = None
        for c in BOTH:
            start, rows = CUTS[c]
            error = result[b][c][core * 4 + zh] - blocks[b, core * 4 + zh, start : start + rows]
            by_row = jnp.sum(error * error, axis=1, keepdims=True)
            row = start + lax.broadcasted_iota(jnp.int32, (rows, TILE), 0)
            column = lax.broadcasted_iota(jnp.int32, (rows, TILE), 1)
            part = jnp.sum(jnp.where(row == column, by_row, 0.0), axis=0, keepdims=True)
            line = part if line is None else line + part
        return jnp.broadcast_to(line, (8, TILE))

    def exchange(stage, first_slot, those):
        return [
            s.start(squares.at[stage], square_in.at[first_slot + i], peer)
            for i, peer in enumerate(those)
        ]

    def collect(stage, first_slot, copies):
        value = squares[stage]
        for i, copy in enumerate(copies):
            copy.wait_recv()
            value = value + square_in[first_slot + i]
        squares[stage + 1] = value

    reduces = [reduce_steps(b) for b in BOTH]
    gathers = [gather_steps(b) for b in BOTH]
    columns = [column_steps(b) for b in BOTH]

    def go(*those):
        for steps in those:
            next(steps, None)

    r0, r1 = reduces
    g0, g1 = gathers
    z0, z1 = columns
    go(r0)
    for copy in dec_copies:
        copy.wait()

    @pl.loop(0, CAP)
    def _(k):
        right[k] = stacked_tile(dec_held[k])

    go(r0, r0, r0, r0, r1, r0, r1, r0, g0, r1, g0, r1, g0, r1, g0, r1, g0, r1, g1)
    go(g0, g1, g0, g1, g0)
    decode(0)
    go(z0, g1, z0, g1, z0, g1, z0, g1, z0, g1)
    go(z0)
    decode(1)
    go(z1, z1, z0, z1, z0, z1)
    squares[0] = own_squares(0) + own_squares(1)
    copies = exchange(0, 0, lines[0])
    collect(0, 0, copies)
    copies = exchange(1, 3, lines[1])
    go(z1)
    collect(1, 3, copies)
    copies = exchange(2, 6, stack)
    go(z1)
    collect(2, 6, copies)
    rms[...] = jnp.sqrt(squares[3] * (1.0 / TOTAL_POINTS) + EPSILON)
    go(z1)
    for steps in (*reduces, *gathers, *columns):
        for _ in steps:
            raise ValueError("steps left")
    assert s.count == N_SEMS
    s.finish()


def assemble_kernel(result_00, result_01, result_10, result_11, rms, out, rms_out):
    result = ((result_00, result_01), (result_10, result_11))
    for i in range(SRC_BLK):
        for b in BOTH:
            for c in BOTH:
                start, rows = CUTS[c]
                out[pl.ds(i * ROWS + start * 2 + b, rows, stride=2)] = result[b][c][i]
    rms_out[...] = rms[0:1, 0:CH]


VMEM = pl.BlockSpec(memory_space=pltpu.VMEM)
HBM = pl.BlockSpec(memory_space=pltpu.HBM)
SMEM = pl.BlockSpec(memory_space=pltpu.SMEM)


def coloured(*lead):
    return [pltpu.VMEM((*lead, rows, TILE), jnp.float32) for _, rows in CUTS]


def pieces(*lead):
    return [coloured(*lead) for _ in BOTH]


def body(
    source_field,
    hidden_gain,
    enc_tiles,
    enc_src_block,
    enc_hid_block,
    enc_count,
    dec_tiles,
    dec_src_block,
    dec_hid_block,
    dec_count,
):
    rows = source_field.transpose(0, 2, 1, 3).reshape(SRC_BLK * ROWS, TILE)
    held = pltpu.VMEM((CAP, TILE, TILE), jnp.float32)
    parts = pl.pallas_call(
        whole_kernel,
        out_shape=(
            *coloured(SRC_BLK),
            *coloured(SRC_BLK),
            pltpu.VMEM((8, TILE), jnp.float32),
        ),
        in_specs=[HBM, HBM, SMEM, HBM, HBM, SMEM, HBM, HBM, HBM, HBM],
        out_specs=(VMEM,) * 5,
        scratch_shapes=[
            pltpu.SMEM((CAP,), jnp.int32),
            pltpu.VMEM((1, CAP), jnp.int32),
            pltpu.VMEM((1, CAP), jnp.int32),
            pltpu.SMEM((CAP,), jnp.int32),
            pltpu.VMEM((SRC_BLK * ROWS, TILE), jnp.float32),
            pltpu.VMEM((1, CH), jnp.float32),
            held,
            held,
            pltpu.VMEM((CAP, TILE), jnp.int32),
            pltpu.SMEM((CAP, TILE), jnp.int32),
            pltpu.VMEM((BATCH, SRC_BLK, CH, TILE), jnp.float32),
            pltpu.VMEM((SRC_BLK, STEP + CH, 2 * TILE), jnp.bfloat16),
            pltpu.VMEM((CAP, 2 * TILE, 2 * TILE), jnp.bfloat16),
            pltpu.VMEM((CAP + 1, STEP + CH, TILE), jnp.float32),
            pieces(HID_BLK),
            pieces(4, 6),
            pieces(8),
            pieces(4),
            pieces(4),
            [[pltpu.VMEM((6, 32, TILE), jnp.float32)] * 2] * 2,
            pieces(),
            pieces(HID_BLK),
            pieces(SRC_BLK),
            pieces(4),
            pieces(4),
            pieces(3),
            pltpu.VMEM((4, 8, TILE), jnp.float32),
            pltpu.VMEM((21, 8, TILE), jnp.float32),
            pltpu.SemaphoreType.DMA((4, 8)),
            pltpu.SemaphoreType.DMA((N_SEMS,)),
            pltpu.SemaphoreType.DMA((N_SEMS,)),
        ],
        compiler_params=pltpu.CompilerParams(collective_id=0, has_side_effects=True),
    )(
        enc_src_block,
        enc_hid_block.reshape(1, CAP),
        enc_count,
        dec_src_block.reshape(1, CAP),
        dec_hid_block,
        dec_count,
        rows,
        hidden_gain.reshape(1, CH),
        enc_tiles,
        dec_tiles,
    )
    returned, rms = pl.pallas_call(
        assemble_kernel,
        out_shape=(
            jax.ShapeDtypeStruct((SRC_BLK * ROWS, TILE), jnp.float32),
            jax.ShapeDtypeStruct((1, CH), jnp.float32),
        ),
        in_specs=[VMEM] * 5,
        out_specs=(VMEM, VMEM),
    )(*[pltpu.with_memory_space_constraint(part, pltpu.VMEM) for part in parts])
    returned = returned.reshape(SRC_BLK, CH, BATCH, TILE).transpose(0, 2, 1, 3)
    return returned, rms.reshape(CH)


def solution(mesh):
    split = Mesh(mesh.devices.reshape(4, 2, 4, 4, 2), AXES)
    every = P(AXES)
    in_specs = (
        P(SRC, None, None, None),
        P(),
        P(AXES, None, None),
        every,
        every,
        every,
        P(AXES, None, None),
        every,
        every,
        every,
    )
    out_specs = (P(SRC, None, None, None), P())
    return jax.shard_map(body, mesh=split, in_specs=in_specs, out_specs=out_specs, check_vma=False)
```

time: 85.6 us -> 105 us (1.23)
  Pallas kernels: 83 us -> 103 us
    pallas_call x1, Pallas kernels: 82.1 us -> 102 us  [body(): pl.pallas_call(whole_kernel, out_shape=(*coloured(SRC_BLK), *coloured(SRC...]
where the time goes in v5:
time: 105 us
  Pallas kernels  103 us (98%)
  between operations  1.93 us (2%)
    pallas_call x1, Pallas kernels, body(): pl.pallas_call(whole_kernel, out_shape=(*coloured(SRC_BLK), *coloured(SRC...  102 us

profile of v5, /device:TPU:1, one launch (start us, length us, event | category | flops | bytes accessed | tf_op | source)
XLA Modules:
  0.0 105.1 jit_solution(17303592013567300214)
XLA Ops:
  1.9 102.2 %shard_map.113 = (f32[8,48,128]{2,1,0:T(8,128)S(1)}, f32[8,50,128]{2,1,0:T(8,128)S(1)}, f32[8,48,128]{2,1,0:T(8,128)S(1)}, f32[8,50,128]{2,1,0:T(8,128)S(1)}, f32[8,128]{1,0:T(8,128)S(1)}) custom-call(s32[32]{0:T(128)} %enc_src_any.1, s32[1,32]{1,0:T(1,128)} %bitcast.11, s32[1]{0:T(128)S(6)} %copy.12.enc_count, s32[1,32]{1,0:T(1,128)} %bitcast.12, ...), custom_call_target="tpu_custom_call" | custom-call | tf_op jit(solution)/shard_map/pallas_call | solution.py:658
  104.1 0.9 shard_map.114

commit v6 on v5

--- a/solution.py
+++ b/solution.py
@@ -22,12 +22,11 @@
 MESH = pl.DeviceIdType.MESH
 TILE_DMAS = 4
 UNROLL = 4
-N_SEMS = 341
+N_SEMS = 200
 
 X, Z, Y, ZH, CORE = AXES
-STEP = 112
-CUTS = ((0, 48), (48, 50))
-HALF = 24
+CUTS = ((0, 96), (96, 100))
+HALF = 48
 COLOURS = ((X, Y), (Y, X))
 BOTH = (0, 1)
 ORDER = (2, 1, 3, 0)
@@ -177,10 +176,8 @@
     gain_any,
     enc_tiles,
     dec_tiles,
-    result_00,
-    result_01,
-    result_10,
-    result_11,
+    result_0,
+    result_1,
     rms,
     enc_src,
     enc_hid,
@@ -202,7 +199,6 @@
     pair_in,
     pair_sum,
     second_in,
-    second_sum,
     hidden,
     back,
     core_in,
@@ -214,13 +210,15 @@
     send_sems,
     recv_sems,
 ):
-    result = ((result_00, result_01), (result_10, result_11))
+    result = (result_0, result_1)
     x, y, z = lax.axis_index(X), lax.axis_index(Y), lax.axis_index(Z)
     zh, core = lax.axis_index(ZH), lax.axis_index(CORE)
     other, twin = 1 - z, 1 - core
     where = {X: x, Y: y}
 
-    lines = [[{axis: shifted(axis, i)} for i in (1, 2, 3)] for axis in (X, Y)]
+    plane = [
+        {X: shifted(X, dx), Y: shifted(Y, dy)} for dx in range(4) for dy in range(4) if dx + dy
+    ]
     stack = [
         {Z: lax.rem(z + dz, 2), ZH: lax.rem(zh + dh, 4), CORE: lax.rem(core + dc, 2)}
         for dz in range(2)
@@ -228,7 +226,7 @@
         for dc in range(2)
         if dz + dh + dc
     ]
-    peers = lines[0] + lines[1] + stack
+    peers = plane + stack
     barrier = pltpu.get_barrier_semaphore()
     small = [
         pltpu.make_async_copy(there, here, local_sems.at[2, i])
@@ -250,7 +248,7 @@
     for peer in peers:
         pl.semaphore_signal(barrier, inc=1, device_id=peer, device_id_type=MESH)
 
-    sums[NONE] = jnp.zeros((STEP + CH, TILE), jnp.float32)
+    sums[NONE] = jnp.zeros((ROWS, TILE), jnp.float32)
     for copy in small:
         copy.wait()
     before, last = chain(enc_hid[...] & (HID_BLK - 1), enc_count[0])
@@ -262,11 +260,9 @@
     table_copy = pltpu.make_async_copy(table, table_s, local_sems.at[3, 0])
     field_copy.wait()
     for i in range(SRC_BLK):
-        left[i, CH:STEP] = jnp.zeros((STEP - CH, 2 * TILE), jnp.bfloat16)
-        for b in BOTH:
-            value = field[pl.ds(i * ROWS + b, CH, stride=2)]
-            blocks[b, i] = value
-            left[i, b * STEP : b * STEP + CH] = split_pair(value)
+        value = field[i * ROWS : (i + 1) * ROWS]
+        blocks[i] = value
+        left[i] = split_pair(value)
         if i == 1:
             table_copy.start()
     for copy in dec_copies:
@@ -286,57 +282,47 @@
     def _(slot):
         for c in BOTH:
             start, rows = CUTS[c]
-            k = table_s[block_in(slot, c), 1]
-            for b in BOTH:
-                partial[b][c][slot] = sums[k, b * STEP + start : b * STEP + start + rows]
+            partial[c][slot] = sums[table_s[block_in(slot, c), 1], start : start + rows]
 
     pl.semaphore_wait(barrier, len(peers))
     s = Sender(send_sems, recv_sems)
-    identity = lax.broadcasted_iota(jnp.int32, (CH, CH), 0) == lax.broadcasted_iota(
-        jnp.int32, (CH, CH), 1
+    row = lax.broadcasted_iota(jnp.int32, (ROWS, CH), 0)
+    column = lax.broadcasted_iota(jnp.int32, (ROWS, CH), 1)
+    scale = jnp.sum(
+        jnp.where((row >> 1) == column, jnp.broadcast_to(gain[...], (ROWS, CH)), 0.0),
+        axis=1,
+        keepdims=True,
     )
-    scale = jnp.sum(
-        jnp.where(identity, jnp.broadcast_to(gain[...], (CH, CH)), 0.0), axis=1, keepdims=True
-    )
-
-    def reduce_steps(b):
+
+    def reduce_steps():
         def first_ring(c, i):
             p, q = COLOURS[c]
             there = shifted(q, ORDER[i])
             return RingSum(
                 s,
                 p,
-                lambda m, h: partial[b][c].at[m * 8 + there * 2 + h],
-                lambda n: first_in[b][c].at[i, n],
-                lambda h: first_sum[b][c].at[there * 2 + h],
+                lambda m, h: partial[c].at[m * 8 + there * 2 + h],
+                lambda n: first_in[c].at[i, n],
+                lambda h: first_sum[c].at[there * 2 + h],
             )
 
-        def second_ring(c):
-            rows = CUTS[c][1]
-            return RingSum(
-                s,
-                COLOURS[c][1],
-                lambda m, h: part_rows(pair_sum[b][c].at[m], h, rows),
-                lambda n: second_in[b][c].at[n, pl.ds(0, rows - HALF if n in (1, 2, 5) else HALF)],
-                lambda h: part_rows(second_sum[b][c], h, rows),
-            )
-
         first = [[first_ring(c, i) for i in range(4)] for c in BOTH]
-        second = [second_ring(c) for c in BOTH]
-        pairs = {}
+        pairs, second = {}, {}
 
         def settle(i):
             for c in BOTH:
                 first[c][i].end()
                 there = shifted(COLOURS[c][1], ORDER[i])
                 pairs[c, i] = s.start(
-                    first_sum[b][c].at[there * 2 + other], pair_in[b][c].at[there], {Z: other}
+                    first_sum[c].at[there * 2 + other], pair_in[c].at[there], {Z: other}
                 )
 
         def pair_back(c, i):
             there = shifted(COLOURS[c][1], ORDER[i])
             pairs[c, i].wait_recv()
-            pair_sum[b][c][there] = first_sum[b][c][there * 2 + z] + pair_in[b][c][there]
+            pair_sum[c][there] = first_sum[c][there * 2 + z] + pair_in[c][there]
+            if i < 3:
+                second[c, i] = s.start(pair_sum[c].at[there], second_in[c].at[i], {COLOURS[c][1]: there})
 
         for i in (0, 1):
             for c in BOTH:
@@ -356,47 +342,49 @@
         settle(1)
         for c in BOTH:
             pair_back(c, 0)
-            second[c].begin_far()
         yield
         for c in BOTH:
             first[c][3].middle()
         settle(2)
         for c in BOTH:
             pair_back(c, 1)
-            second[c].begin_right()
-            second[c].middle_right()
         yield
         settle(3)
         for c in BOTH:
             pair_back(c, 2)
-            second[c].begin_left()
-            second[c].middle_left()
-        yield
-        squares_sum = None
+        yield
+        evens, odds, values = [], [], []
         for c in BOTH:
             pair_back(c, 3)
-            second[c].end()
-            value = second_sum[b][c][...]
-            square = jnp.sum(value * value, axis=0, keepdims=True)
-            squares_sum = square if squares_sum is None else squares_sum + square
-        factor = lax.rsqrt(squares_sum * (1.0 / CH) + EPSILON)
+            value = pair_sum[c][where[COLOURS[c][1]]]
+            for i in range(3):
+                second[c, i].wait_recv()
+                value = value + second_in[c][i]
+            values.append(value)
+            parity = lax.broadcasted_iota(jnp.int32, value.shape, 0) & 1
+            square = value * value
+            evens.append(jnp.sum(jnp.where(parity == 0, square, 0.0), axis=0, keepdims=True))
+            odds.append(jnp.sum(jnp.where(parity == 1, square, 0.0), axis=0, keepdims=True))
+        even = lax.rsqrt((evens[0] + evens[1]) * (1.0 / CH) + EPSILON)
+        odd = lax.rsqrt((odds[0] + odds[1]) * (1.0 / CH) + EPSILON)
         for c in BOTH:
             start, rows = CUTS[c]
+            parity = lax.broadcasted_iota(jnp.int32, (rows, TILE), 0) & 1
             p, q = (where[axis] for axis in COLOURS[c])
-            hidden[b][c][p * 8 + q * 2 + z] = (
-                second_sum[b][c][...] * scale[start : start + rows] * factor
+            hidden[c][p * 8 + q * 2 + z] = (
+                values[c] * scale[start : start + rows] * jnp.where(parity == 0, even, odd)
             )
 
-    def gather_steps(b):
+    def gather_steps():
         inner, paired, outer, passed = {}, {}, {}, {}
 
         def outer_block(c, m, step, far):
             there = shifted(COLOURS[c][1], step)
-            return hidden[b][c].at[m * 8 + there * 2 + (other if far else z)]
+            return hidden[c].at[m * 8 + there * 2 + (other if far else z)]
 
         def inner_block(c, step):
             p, q = COLOURS[c]
-            return hidden[b][c].at[where[p] * 8 + shifted(q, step) * 2 + z]
+            return hidden[c].at[where[p] * 8 + shifted(q, step) * 2 + z]
 
         def to_pair(c, step):
             paired[c, step] = s.along(inner_block(c, step), Z, 1)
@@ -418,98 +406,71 @@
 
         for c in BOTH:
             q, mine = COLOURS[c][1], inner_block(c, 0)
-            inner[c] = [s.along(mine, q, 1), s.along(mine, q, -1)]
+            for step in (1, 3, 2):
+                inner[c, step] = s.along(mine, q, step)
             to_pair(c, 0)
         for c in BOTH:
             to_line(c, 0, False)
         yield
-        for c in BOTH:
-            q, rows = COLOURS[c][1], CUTS[c][1]
-            from_left, from_right = inner[c]
-            from_left.wait_recv()
-            inner[c] = [s.along(part_rows(inner_block(c, -1), 0, rows), q, 1)]
-            to_pair(c, -1)
-            from_right.wait_recv()
-            inner[c].append(s.along(part_rows(inner_block(c, 1), 1, rows), q, -1))
-            to_pair(c, 1)
-            to_line(c, -1, False)
-            to_line(c, 1, False)
+        for step in (1, 3, 2):
+            for c in BOTH:
+                inner[c, step].wait_recv()
+                to_pair(c, 4 - step)
+                to_line(c, 4 - step, False)
         yield
         for c in BOTH:
             paired[c, 0].wait_recv()
             to_line(c, 0, True)
+        yield
         for c in BOTH:
             along_line(c, 0, False)
         yield
-        for c in BOTH:
-            for copy in inner[c]:
-                copy.wait_recv()
-            to_pair(c, 2)
-            to_line(c, 2, False)
-        yield
-        for c in BOTH:
-            for step in (-1, 1):
+        for step in (3, 1, 2):
+            for c in BOTH:
                 paired[c, step].wait_recv()
                 to_line(c, step, True)
-        for c in BOTH:
-            along_line(c, -1, False)
-            along_line(c, 1, False)
-            along_line(c, 0, True)
-        yield
-        for c in BOTH:
-            paired[c, 2].wait_recv()
-            to_line(c, 2, True)
-        for c in BOTH:
-            along_line(c, 2, False)
-            along_line(c, -1, True)
-            along_line(c, 1, True)
-        yield
-        for c in BOTH:
-            along_line(c, 2, True)
+        yield
+        for step, far in ((3, False), (1, False), (0, True), (2, False), (3, True), (1, True), (2, True)):
+            for c in BOTH:
+                along_line(c, step, far)
         yield
         for c, step, far in passed:
             outer[c, step, far][0 if far else 1].wait_recv()
             passed[c, step, far].wait_recv()
 
-    def decode(b):
+    def decode(c):
+        here = slice(CUTS[c][0], CUTS[c][0] + CUTS[c][1])
+
         @pl.loop(0, CAP // UNROLL)
         def _(step):
             for i in range(UNROLL):
                 k = step * UNROLL + i
                 block = dec_hid[k] & (HID_BLK - 1)
-                pieces = [split_pair(hidden[b][c][slot_of(block, c)]) for c in BOTH]
-                product = full_product(jnp.concatenate(pieces, axis=0), right[k])
-                here = slice(b * STEP, b * STEP + CH)
+                product = full_product(split_pair(hidden[c][slot_of(block, c)]), right[k])
                 sums[k, here] = sums[table_s[k, 2], here] + product
 
         @pl.loop(0, SRC_BLK)
         def _(i):
-            k = table_s[i, 3]
-            for c in BOTH:
-                start, rows = CUTS[c]
-                back[b][c][i] = sums[k, b * STEP + start : b * STEP + start + rows]
-
-    def column_steps(b):
+            back[c][i] = sums[table_s[i, 3], here]
+
+    def column_steps(c):
+        rows = CUTS[c][1]
         crossing = {}
         for step in ORDER:
             m = lax.rem(zh + step, 4)
-            for c in BOTH:
-                crossing[step, c] = s.start(
-                    back[b][c].at[twin * 4 + m], core_in[b][c].at[m], {CORE: twin}
-                )
+            crossing[step] = s.start(back[c].at[twin * 4 + m], core_in[c].at[m], {CORE: twin})
         yield
         ring = RingSum(
             s,
             ZH,
-            lambda m, h: core_sum[b][h].at[m],
-            lambda n: ring_in[b][(0, 1, 1, 0, 0, 1)[n]].at[(0, 0, 1, 1, 2, 2)[n]],
-            lambda h: result[b][h].at[core * 4 + zh],
+            lambda m, h: part_rows(core_sum[c].at[m], h, rows),
+            lambda n: ring_in[c].at[n, pl.ds(0, rows - HALF if n in (1, 2, 5) else HALF)],
+            lambda h: part_rows(result[c].at[core * 4 + zh], h, rows),
         )
         for step in ORDER:
             m = lax.rem(zh + step, 4)
-            for c in BOTH:
-                crossing[step, c].wait_recv()
-                core_sum[b][c][m] = back[b][c][core * 4 + m] + core_in[b][c][m]
+            crossing[step].wait_recv()
+            core_sum[c][m] = back[c][core * 4 + m] + core_in[c][m]
             if step == 2:
                 ring.begin_far()
             elif step == 1:
@@ -522,16 +483,16 @@
         ring.end()
 
         def own_half(step, h):
-            return result[b][h].at[core * 4 + lax.rem(zh + step, 4)]
-
-        def to_twin(step, c):
-            return s.along(own_half(step, c), CORE, 1)
+            return part_rows(result[c].at[core * 4 + lax.rem(zh + step, 4)], h, rows)
+
+        def to_twin(step, h):
+            return s.along(own_half(step, h), CORE, 1)
 
         to_right = [s.along(own_half(0, 0), ZH, 1)]
         to_left = [s.along(own_half(0, 1), ZH, -1)]
         to_right.append(s.along(own_half(0, 1), ZH, 1))
         to_left.append(s.along(own_half(0, 0), ZH, -1))
-        twins = [to_twin(0, c) for c in BOTH]
+        twins = [s.along(result[c].at[core * 4 + zh], CORE, 1)]
         yield
         to_right[0].wait_recv()
         passing = [s.along(own_half(3, 0), ZH, 1)]
@@ -542,23 +503,20 @@
         to_right[1].wait_recv()
         to_left[1].wait_recv()
         twins += [to_twin(3, 1), to_twin(1, 0)]
-        for c in BOTH:
-            passing[c].wait_recv()
-            twins.append(to_twin(2, c))
+        for h in BOTH:
+            passing[h].wait_recv()
+            twins.append(to_twin(2, h))
         yield
         for copy in twins:
             copy.wait_recv()
 
-    def own_squares(b):
-        line = None
-        for c in BOTH:
-            start, rows = CUTS[c]
-            error = result[b][c][core * 4 + zh] - blocks[b, core * 4 + zh, start : start + rows]
-            by_row = jnp.sum(error * error, axis=1, keepdims=True)
-            row = start + lax.broadcasted_iota(jnp.int32, (rows, TILE), 0)
-            column = lax.broadcasted_iota(jnp.int32, (rows, TILE), 1)
-            part = jnp.sum(jnp.where(row == column, by_row, 0.0), axis=0, keepdims=True)
-            line = part if line is None else line + part
+    def own_squares(c):
+        start, rows = CUTS[c]
+        error = result[c][core * 4 + zh] - blocks[core * 4 + zh, start : start + rows]
+        by_row = jnp.sum(error * error, axis=1, keepdims=True)
+        row = start + lax.broadcasted_iota(jnp.int32, (rows, TILE), 0)
+        column = lax.broadcasted_iota(jnp.int32, (rows, TILE), 1)
+        line = jnp.sum(jnp.where((row >> 1) == column, by_row, 0.0), axis=0, keepdims=True)
         return jnp.broadcast_to(line, (8, TILE))
 
     def exchange(stage, first_slot, those):
@@ -574,18 +532,15 @@
             value = value + square_in[first_slot + i]
         squares[stage + 1] = value
 
-    reduces = [reduce_steps(b) for b in BOTH]
-    gathers = [gather_steps(b) for b in BOTH]
-    columns = [column_steps(b) for b in BOTH]
+    columns = [column_steps(c) for c in BOTH]
+    reduce, gather = reduce_steps(), gather_steps()
 
     def go(*those):
         for steps in those:
             next(steps, None)
 
-    r0, r1 = reduces
-    g0, g1 = gathers
     z0, z1 = columns
-    go(r0)
+    go(reduce)
     for copy in dec_copies:
         copy.wait()
 
@@ -593,38 +548,32 @@
     def _(k):
         right[k] = stacked_tile(dec_held[k])
 
-    go(r0, r0, r0, r0, r1, r0, r1, r0, g0, r1, g0, r1, g0, r1, g0, r1, g0, r1, g1)
-    go(g0, g1, g0, g1, g0)
+    for steps in (reduce, gather):
+        for _ in steps:
+            pass
     decode(0)
-    go(z0, g1, z0, g1, z0, g1, z0, g1, z0, g1)
     go(z0)
     decode(1)
-    go(z1, z1, z0, z1, z0, z1)
-    squares[0] = own_squares(0) + own_squares(1)
-    copies = exchange(0, 0, lines[0])
+    go(z1, z0, z1, z0, z1, z0, z1)
+    line = own_squares(0)
+    go(z0)
+    squares[0] = line + own_squares(1)
+    copies = exchange(0, 0, plane)
+    go(z1)
     collect(0, 0, copies)
-    copies = exchange(1, 3, lines[1])
-    go(z1)
-    collect(1, 3, copies)
-    copies = exchange(2, 6, stack)
-    go(z1)
-    collect(2, 6, copies)
-    rms[...] = jnp.sqrt(squares[3] * (1.0 / TOTAL_POINTS) + EPSILON)
-    go(z1)
-    for steps in (*reduces, *gathers, *columns):
-        for _ in steps:
-            raise ValueError("steps left")
+    copies = exchange(1, 15, stack)
+    go(z0, z1)
+    collect(1, 15, copies)
+    rms[...] = jnp.sqrt(squares[2] * (1.0 / TOTAL_POINTS) + EPSILON)
+    go(z0, z1)
     assert s.count == N_SEMS
     s.finish()
 
 
-def assemble_kernel(result_00, result_01, result_10, result_11, rms, out, rms_out):
-    result = ((result_00, result_01), (result_10, result_11))
+def assemble_kernel(result_0, result_1, rms, out, rms_out):
     for i in range(SRC_BLK):
-        for b in BOTH:
-            for c in BOTH:
-                start, rows = CUTS[c]
-                out[pl.ds(i * ROWS + start * 2 + b, rows, stride=2)] = result[b][c][i]
+        for (start, rows), part in zip(CUTS, (result_0, result_1)):
+            out[i * ROWS + start : i * ROWS + start + rows] = part[i]
     rms_out[...] = rms[0:1, 0:CH]
 
 
@@ -635,10 +584,6 @@
 
 def coloured(*lead):
     return [pltpu.VMEM((*lead, rows, TILE), jnp.float32) for _, rows in CUTS]
-
-
-def pieces(*lead):
-    return [coloured(*lead) for _ in BOTH]
 
 
 def body(
@@ -659,11 +604,10 @@
         whole_kernel,
         out_shape=(
             *coloured(SRC_BLK),
-            *coloured(SRC_BLK),
             pltpu.VMEM((8, TILE), jnp.float32),
         ),
         in_specs=[HBM, HBM, SMEM, HBM, HBM, SMEM, HBM, HBM, HBM, HBM],
-        out_specs=(VMEM,) * 5,
+        out_specs=(VMEM,) * 3,
         scratch_shapes=[
             pltpu.SMEM((CAP,), jnp.int32),
             pltpu.VMEM((1, CAP), jnp.int32),
@@ -675,24 +619,23 @@
             held,
             pltpu.VMEM((CAP, TILE), jnp.int32),
             pltpu.SMEM((CAP, TILE), jnp.int32),
-            pltpu.VMEM((BATCH, SRC_BLK, CH, TILE), jnp.float32),
-            pltpu.VMEM((SRC_BLK, STEP + CH, 2 * TILE), jnp.bfloat16),
+            pltpu.VMEM((SRC_BLK, ROWS, TILE), jnp.float32),
+            pltpu.VMEM((SRC_BLK, ROWS, 2 * TILE), jnp.bfloat16),
             pltpu.VMEM((CAP, 2 * TILE, 2 * TILE), jnp.bfloat16),
-            pltpu.VMEM((CAP + 1, STEP + CH, TILE), jnp.float32),
-            pieces(HID_BLK),
-            pieces(4, 6),
-            pieces(8),
-            pieces(4),
-            pieces(4),
-            [[pltpu.VMEM((6, 32, TILE), jnp.float32)] * 2] * 2,
-            pieces(),
-            pieces(HID_BLK),
-            pieces(SRC_BLK),
-            pieces(4),
-            pieces(4),
-            pieces(3),
-            pltpu.VMEM((4, 8, TILE), jnp.float32),
-            pltpu.VMEM((21, 8, TILE), jnp.float32),
+            pltpu.VMEM((CAP + 1, ROWS, TILE), jnp.float32),
+            coloured(HID_BLK),
+            coloured(4, 6),
+            coloured(8),
+            coloured(4),
+            coloured(4),
+            coloured(3),
+            coloured(HID_BLK),
+            coloured(SRC_BLK),
+            coloured(4),
+            coloured(4),
+            [pltpu.VMEM((6, 56, TILE), jnp.float32)] * 2,
+            pltpu.VMEM((3, 8, TILE), jnp.float32),
+            pltpu.VMEM((30, 8, TILE), jnp.float32),
             pltpu.SemaphoreType.DMA((4, 8)),
             pltpu.SemaphoreType.DMA((N_SEMS,)),
             pltpu.SemaphoreType.DMA((N_SEMS,)),
@@ -716,7 +659,7 @@
             jax.ShapeDtypeStruct((SRC_BLK * ROWS, TILE), jnp.float32),
             jax.ShapeDtypeStruct((1, CH), jnp.float32),
         ),
-        in_specs=[VMEM] * 5,
+        in_specs=[VMEM] * 3,
         out_specs=(VMEM, VMEM),
     )(*[pltpu.with_memory_space_constraint(part, pltpu.VMEM) for part in parts])
     returned = returned.reshape(SRC_BLK, CH, BATCH, TILE).transpose(0, 2, 1, 3)

time: 105 us -> 87.1 us (0.83)
  Pallas kernels: 103 us -> 85 us
    pallas_call x1, Pallas kernels: 102 us -> 84.1 us  [body(): pl.pallas_call(whole_kernel, out_shape=(*coloured(SRC_BLK), pltpu.VMEM((8...]
where the time goes in v6:
time: 87.1 us; the launch traced here: 86.9 us
  Pallas kernels  85 us (98%)
  between operations  1.93 us (2%)
    pallas_call x1, Pallas kernels, body(): pl.pallas_call(whole_kernel, out_shape=(*coloured(SRC_BLK), pltpu.VMEM((8...  84.1 us

profile of v6, /device:TPU:1, one launch (start us, length us, event | category | flops | bytes accessed | tf_op | source)
XLA Modules:
  0.0 86.9 jit_solution(3902369132344179727)
XLA Ops:
  1.9 84.1 %shard_map.113 = (f32[8,96,128]{2,1,0:T(8,128)S(1)}, f32[8,100,128]{2,1,0:T(8,128)S(1)}, f32[8,128]{1,0:T(8,128)S(1)}) custom-call(s32[32]{0:T(128)} %enc_src_any.1, s32[1,32]{1,0:T(1,128)} %bitcast.11, s32[1]{0:T(128)S(6)} %copy.12.enc_count, s32[1,32]{1,0:T(1,128)} %bitcast.12, s32[32]{0:T(128)} %dec_hid_any.1, s32[1]{0:T(128)S(6)} %copy.13.dec_count, ...), custom_call_target="tpu_custom_call" | custom-call | tf_op jit(solution)/shard_map/pallas_call | solution.py:603
  86.0 0.9 %shard_map.114 = (f32[1568,128]{1,0:T(8,128)}, f32[1,98]{1,0:T(1,128)}) custom-call(f32[8,96,128]{2,1,0:T(8,128)S(1)} %get-tuple-element.7.result_0, f32[8,100,128]{2,1,0:T(8,128)S(1)} %get-tuple-element.8.result_1, f32[8,128]{1,0:T(8,128)S(1)} %get-tuple-element.9.rms), custom_call_target="tpu_custom_call" | custom-call | tf_op jit(solution)/shard_map/pallas_call | solution.py:656

commit v7 on v6

--- a/solution.py
+++ b/solution.py
@@ -20,9 +20,9 @@
 SRC = ("src_0", "src_1", "src_2")
 SIZES = {"src_0": 4, "src_1": 2, "src_2": 4, "hid_0": 4, "hid_1": 2}
 MESH = pl.DeviceIdType.MESH
-TILE_DMAS = 4
-UNROLL = 4
-N_SEMS = 200
+TILE_DMAS = 2
+UNROLL = 16
+N_SEMS = 188
 
 X, Z, Y, ZH, CORE = AXES
 CUTS = ((0, 96), (96, 100))
@@ -159,10 +159,6 @@
         self.total(0)[...] = (part(me, 0)[...] + landed(3)[...]) + landed(4)[...]
         self.l3.wait_recv()
         self.total(1)[...] = (part(me, 1)[...] + landed(2)[...]) + landed(5)[...]
-
-
-def part_rows(ref, h, rows):
-    return ref.at[pl.ds(h * HALF, rows - HALF if h else HALF)]
 
 
 def whole_kernel(
@@ -324,21 +320,28 @@
             if i < 3:
                 second[c, i] = s.start(pair_sum[c].at[there], second_in[c].at[i], {COLOURS[c][1]: there})
 
-        for i in (0, 1):
-            for c in BOTH:
-                first[c][i].begin()
+        for c in BOTH:
+            first[c][0].begin()
+        for c in BOTH:
+            first[c][1].begin_far()
         yield
         for c in BOTH:
             first[c][0].middle()
-            first[c][2].begin()
+            first[c][2].begin_far()
+            first[c][1].begin_right()
+            first[c][1].begin_left()
         yield
         for c in BOTH:
             first[c][1].middle()
-            first[c][3].begin()
+            first[c][3].begin_far()
+            first[c][2].begin_right()
+            first[c][2].begin_left()
         settle(0)
         yield
         for c in BOTH:
             first[c][2].middle()
+            first[c][3].begin_right()
+            first[c][3].begin_left()
         settle(1)
         for c in BOTH:
             pair_back(c, 0)
@@ -438,35 +441,37 @@
             outer[c, step, far][0 if far else 1].wait_recv()
             passed[c, step, far].wait_recv()
 
-    def decode(c):
-        here = slice(CUTS[c][0], CUTS[c][0] + CUTS[c][1])
-
-        @pl.loop(0, CAP // UNROLL)
-        def _(step):
-            for i in range(UNROLL):
-                k = step * UNROLL + i
-                block = dec_hid[k] & (HID_BLK - 1)
-                product = full_product(split_pair(hidden[c][slot_of(block, c)]), right[k])
-                sums[k, here] = sums[table_s[k, 2], here] + product
+    def decode():
+        for k in range(CAP):
+            block = dec_hid[k] & (HID_BLK - 1)
+            split = [split_pair(hidden[c][slot_of(block, c)]) for c in BOTH]
+            product = full_product(jnp.concatenate(split, axis=0), right[k])
+            sums[k] = sums[table_s[k, 2]] + product
 
         @pl.loop(0, SRC_BLK)
         def _(i):
-            back[c][i] = sums[table_s[i, 3], here]
+            for c in BOTH:
+                start, rows = CUTS[c]
+                back[c][i] = sums[table_s[i, 3], start : start + rows]
 
     def column_steps(c):
+        crossing, column, twins = {}, {}, []
         rows = CUTS[c][1]
-        crossing = {}
+
+        def half_of(block, h):
+            return block.at[pl.ds(h * HALF, rows - HALF if h else HALF)]
+
+        ring = RingSum(
+            s,
+            ZH,
+            lambda m, h: half_of(core_sum[c].at[m], h),
+            lambda n: ring_in[c].at[n, pl.ds(0, rows - HALF if n in (1, 2, 5) else HALF)],
+            lambda h: half_of(result[c].at[core * 4 + zh], h),
+        )
         for step in ORDER:
             m = lax.rem(zh + step, 4)
             crossing[step] = s.start(back[c].at[twin * 4 + m], core_in[c].at[m], {CORE: twin})
         yield
-        ring = RingSum(
-            s,
-            ZH,
-            lambda m, h: part_rows(core_sum[c].at[m], h, rows),
-            lambda n: ring_in[c].at[n, pl.ds(0, rows - HALF if n in (1, 2, 5) else HALF)],
-            lambda h: part_rows(result[c].at[core * 4 + zh], h, rows),
-        )
         for step in ORDER:
             m = lax.rem(zh + step, 4)
             crossing[step].wait_recv()
@@ -481,31 +486,14 @@
         ring.middle()
         yield
         ring.end()
-
-        def own_half(step, h):
-            return part_rows(result[c].at[core * 4 + lax.rem(zh + step, 4)], h, rows)
-
-        def to_twin(step, h):
-            return s.along(own_half(step, h), CORE, 1)
-
-        to_right = [s.along(own_half(0, 0), ZH, 1)]
-        to_left = [s.along(own_half(0, 1), ZH, -1)]
-        to_right.append(s.along(own_half(0, 1), ZH, 1))
-        to_left.append(s.along(own_half(0, 0), ZH, -1))
-        twins = [s.along(result[c].at[core * 4 + zh], CORE, 1)]
-        yield
-        to_right[0].wait_recv()
-        passing = [s.along(own_half(3, 0), ZH, 1)]
-        to_left[0].wait_recv()
-        passing.append(s.along(own_half(1, 1), ZH, -1))
-        twins += [to_twin(3, 0), to_twin(1, 1)]
-        yield
-        to_right[1].wait_recv()
-        to_left[1].wait_recv()
-        twins += [to_twin(3, 1), to_twin(1, 0)]
-        for h in BOTH:
-            passing[h].wait_recv()
-            twins.append(to_twin(2, h))
+        mine = result[c].at[core * 4 + zh]
+        for step in (2, 1, 3):
+            column[step] = s.along(mine, ZH, step)
+        twins.append(s.along(mine, CORE, 1))
+        yield
+        for step in (1, 3, 2):
+            column[step].wait_recv()
+            twins.append(s.along(result[c].at[core * 4 + lax.rem(zh + 4 - step, 4)], CORE, 1))
         yield
         for copy in twins:
             copy.wait_recv()
@@ -551,15 +539,12 @@
     for steps in (reduce, gather):
         for _ in steps:
             pass
-    decode(0)
-    go(z0)
-    decode(1)
-    go(z1, z0, z1, z0, z1, z0, z1)
+    decode()
+    go(z0, z1, z0, z1, z0, z1, z0)
     line = own_squares(0)
-    go(z0)
+    go(z1)
     squares[0] = line + own_squares(1)
     copies = exchange(0, 0, plane)
-    go(z1)
     collect(0, 0, copies)
     copies = exchange(1, 15, stack)
     go(z0, z1)

time: 87.1 us -> 81.2 us (0.932)
  Pallas kernels: 85 us -> 78.7 us
    pallas_call x1, Pallas kernels: 84.1 us -> 77.8 us  [body(): pl.pallas_call(whole_kernel, out_shape=(*coloured(SRC_BLK), pltpu.VMEM((8...]
where the time goes in v7:
time: 81.2 us; the launch traced here: 80.7 us
  Pallas kernels  78.7 us (97%)
  between operations  1.93 us (2%)
    pallas_call x1, Pallas kernels, body(): pl.pallas_call(whole_kernel, out_shape=(*coloured(SRC_BLK), pltpu.VMEM((8...  77.8 us

profile of v7, /device:TPU:1, one launch (start us, length us, event | category | flops | bytes accessed | tf_op | source)
XLA Modules:
  0.0 80.7 jit_solution(6591663966964639423)
XLA Ops:
  1.9 77.8 %shard_map.113 = (f32[8,96,128]{2,1,0:T(8,128)S(1)}, f32[8,100,128]{2,1,0:T(8,128)S(1)}, f32[8,128]{1,0:T(8,128)S(1)}) custom-call(s32[32]{0:T(128)} %enc_src_any.1, s32[1,32]{1,0:T(1,128)} %bitcast.11, s32[1]{0:T(128)S(6)} %copy.12.enc_count, s32[1,32]{1,0:T(1,128)} %bitcast.12, s32[32]{0:T(128)} %dec_hid_any.1, s32[1]{0:T(128)S(6)} %copy.13.dec_count, ...), custom_call_target="tpu_custom_call" | custom-call | tf_op jit(solution)/shard_map/pallas_call | solution.py:588
  79.7 0.9 %shard_map.114 = (f32[1568,128]{1,0:T(8,128)}, f32[1,98]{1,0:T(1,128)}) custom-call(f32[8,96,128]{2,1,0:T(8,128)S(1)} %get-tuple-element.7.result_0, f32[8,100,128]{2,1,0:T(8,128)S(1)} %get-tuple-element.8.result_1, f32[8,128]{1,0:T(8,128)S(1)} %get-tuple-element.9.rms), custom_call_target="tpu_custom_call" | custom-call | tf_op jit(solution)/shard_map/pallas_call | solution.py:641

commit v8 on v7

--- a/solution.py
+++ b/solution.py
@@ -487,7 +487,7 @@
         yield
         ring.end()
         mine = result[c].at[core * 4 + zh]
-        for step in (2, 1, 3):
+        for step in (1, 3, 2):
             column[step] = s.along(mine, ZH, step)
         twins.append(s.along(mine, CORE, 1))
         yield
@@ -528,6 +528,7 @@
             next(steps, None)
 
     z0, z1 = columns
+    go(reduce)
     go(reduce)
     for copy in dec_copies:
         copy.wait()

time: 81.2 us -> 80.8 us (level)
  no operation moved by 1% of the time
where the time goes in v8:
time: 80.8 us; the launch traced here: 80.4 us
  Pallas kernels  78.5 us (97%)
  between operations  1.93 us (2%)
    pallas_call x1, Pallas kernels, body(): pl.pallas_call(whole_kernel, out_shape=(*coloured(SRC_BLK), pltpu.VMEM((8...  77.5 us

profile of v8, /device:TPU:1, one launch (start us, length us, event | category | flops | bytes accessed | tf_op | source)
XLA Modules:
  0.0 80.4 jit_solution(16178326894022586443)
XLA Ops:
  1.9 77.5 %shard_map.113 = (f32[8,96,128]{2,1,0:T(8,128)S(1)}, f32[8,100,128]{2,1,0:T(8,128)S(1)}, f32[8,128]{1,0:T(8,128)S(1)}) custom-call(s32[32]{0:T(128)} %enc_src_any.1, s32[1,32]{1,0:T(1,128)} %bitcast.11, s32[1]{0:T(128)S(6)} %copy.12.enc_count, s32[1,32]{1,0:T(1,128)} %bitcast.12, s32[32]{0:T(128)} %dec_hid_any.1, s32[1]{0:T(128)S(6)} %copy.13.dec_count, ...), custom_call_target="tpu_custom_call" | custom-call | tf_op jit(solution)/shard_map/pallas_call | solution.py:589
  79.5 0.9 %shard_map.114 = (f32[1568,128]{1,0:T(8,128)}, f32[1,98]{1,0:T(1,128)}) custom-call(f32[8,96,128]{2,1,0:T(8,128)S(1)} %get-tuple-element.7.result_0, f32[8,100,128]{2,1,0:T(8,128)S(1)} %get-tuple-element.8.result_1, f32[8,128]{1,0:T(8,128)S(1)} %get-tuple-element.9.rms), custom_call_target="tpu_custom_call" | custom-call | tf_op jit(solution)/shard_map/pallas_call | solution.py:642
